TPU v7x, 32 devices: a whole 2x2x4 slice. The times are simulated.
32 devices in a mesh: page: 8 (over z, x), band: 4 (over y, core).
Axes of the slice: x: 2, y: 2, z: 4, core: 2. Of those that a mesh axis runs over, the one named last changes fastest.
Arguments:
- tokens: bfloat16 [32, 512, 768], P('page', 'band'), may hold values from -6 to 6
- band_ids: int32 [32, 512], P('page'), may hold values from 0 to 3, as said below
- band_counts: int32 [32, 4], P('page'), may hold values from 64 to 256, as said below
- page_mask: int32 [32, 512], P('page'), may hold values from 0 to 1, as said below
- w_query: bfloat16 [768, 768], P(('page', 'band')), may hold values from -0.21875 to 0.21875
- b_query: bfloat16 [768], P(('page', 'band')), may hold values from -1.5 to 1.5
- w_key: bfloat16 [768, 768], P(('page', 'band')), may hold values from -0.3125 to 0.3125
- w_value: bfloat16 [768, 768], P(('page', 'band')), may hold values from -0.21875 to 0.21875
- b_value: bfloat16 [768], P(('page', 'band')), may hold values from -0.5 to 0.5
- w_attn_out: bfloat16 [768, 768], P(('page', 'band')), may hold values from -1.25 to 1.25
- b_attn_out: bfloat16 [768], P(('page', 'band')), may hold values from -1 to 1
- attn_gain: bfloat16 [768], P(('page', 'band')), may hold values from 0.5 to 1.5
- attn_shift: bfloat16 [768], P(('page', 'band')), may hold values from -1 to 1
- w_inner: bfloat16 [768, 3072], P(('page', 'band')), may hold values from -0.21875 to 0.21875
- b_inner: bfloat16 [3072], P(('page', 'band')), may hold values from -1 to 1
- w_outer: bfloat16 [3072, 768], P(('page', 'band')), may hold values from -0.109375 to 0.109375
- b_outer: bfloat16 [768], P(('page', 'band')), may hold values from -1 to 1
- ffn_gain: bfloat16 [768], P(('page', 'band')), may hold values from 0.5 to 1.5
- ffn_shift: bfloat16 [768], P(('page', 'band')), may hold values from -1.5 to 1.5
- grad_output: bfloat16 [32, 1024, 768], P('page', 'band'), may hold values from -6 to 6
Outputs:
- layer_out: bfloat16 [32, 1024, 768], P('page', 'band')
- grad_tokens: bfloat16 [32, 512, 768], P('page', 'band')
- grad_w_query: float32 [768, 768], P(('page', 'band'))
- grad_b_query: float32 [768], P(('page', 'band'))
- grad_w_key: float32 [768, 768], P(('page', 'band'))
- grad_w_value: float32 [768, 768], P(('page', 'band'))
- grad_b_value: float32 [768], P(('page', 'band'))
- grad_w_attn_out: float32 [768, 768], P(('page', 'band'))
- grad_b_attn_out: float32 [768], P(('page', 'band'))
- grad_attn_gain: float32 [768], P(('page', 'band'))
- grad_attn_shift: float32 [768], P(('page', 'band'))
- grad_w_inner: float32 [768, 3072], P(('page', 'band'))
- grad_b_inner: float32 [3072], P(('page', 'band'))
- grad_w_outer: float32 [3072, 768], P(('page', 'band'))
- grad_b_outer: float32 [768], P(('page', 'band'))
- grad_ffn_gain: float32 [768], P(('page', 'band'))
- grad_ffn_shift: float32 [768], P(('page', 'band'))
Inputs may be any that keep to these rules, and one draw needn't show every extreme that they name: `band_ids`: in each page every band holds between 64 and 256 tokens; one band holds exactly 256 tokens, 64 in each quarter of the page (128 positions in a row), and another holds exactly 64; no band holds more than 64 tokens of one quarter of a page. band_counts[p, b] is the number of tokens of page p whose band id is b. `page_mask`: in each page the ones form a prefix of at least 128 positions, and the page ends with at least one 0.
All inputs are finite; a program needn't handle non-finite values.
Results may differ from a plain program's by a relative error of at most 0.04.
Values may be sent and summed in bfloat16 or wider, within the bound.
A program may use at most 192 MiB of HBM per device.

v0:
```python
import jax
import jax.numpy as jnp
from jax import lax
from jax.experimental import pallas as pl
from jax.experimental.pallas import tpu as pltpu
from jax.sharding import PartitionSpec as P

HEAD_DIM = 64
LN_EPS = 1e-12
NEG_FILL = -1e30
MESH = pl.DeviceIdType.MESH
DMA = pltpu.SemaphoreType.DMA
F32 = jnp.float32
BF16 = jnp.bfloat16
BOTH = ("page", "band")
VMEM_LIMIT = 62 * 2**20


def my_place():
    page, band = lax.axis_index("page"), lax.axis_index("band")
    return page // 2, page % 2, band // 2, band % 2


def dev(z, x, y, c):
    return (z * 2 + x, y * 2 + c)


def remote(src, dst, send_sem, recv_sem, place):
    return pltpu.make_async_remote_copy(
        src_ref=src,
        dst_ref=dst,
        send_sem=send_sem,
        recv_sem=recv_sem,
        device_id=dev(*place),
        device_id_type=MESH,
    )


def meet(places):
    barrier = pltpu.get_barrier_semaphore()
    for place in places:
        pl.semaphore_signal(barrier, inc=1, device_id=dev(*place), device_id_type=MESH)
    pl.semaphore_wait(barrier, len(places))


def grid_peers(z, x, y, c):
    return [((z + j) % 4, x, y, c) for j in (1, 2, 3)] + [
        (z, 1 - x, y, c),
        (z, x, 1 - y, c),
        (z, x, y, 1 - c),
    ]


def half(ref, which):
    rows, width = ref.shape[-2] // 2, ref.shape[-1] // 2
    if width % 128:
        return ref.at[..., pl.ds(which * rows, rows), :]
    return ref.at[..., pl.ds(which * width, width)]


def norm_rows(values):
    center = values - jnp.mean(values, axis=-1, keepdims=True)
    factor = lax.rsqrt(jnp.mean(center * center, axis=-1, keepdims=True) + LN_EPS)
    return (center * factor, factor)


def norm_back(upstream, normed, factor):
    return factor * (
        upstream
        - jnp.mean(upstream, axis=-1, keepdims=True)
        - normed * jnp.mean(upstream * normed, axis=-1, keepdims=True)
    )


def dot(first, second):
    return jnp.dot(first, second, preferred_element_type=F32)


def dot_rows(first, second):
    return lax.dot_general(first, second, (((0,), (0,)), ((), ())), preferred_element_type=F32)


def dot_cols(first, second):
    return lax.dot_general(first, second, (((1,), (1,)), ((), ())), preferred_element_type=F32)


def page_slots(ids, bands, slot_cap):
    onehot = (ids[:, :, None] == jnp.arange(bands, dtype=jnp.int32)).astype(F32)
    length = ids.shape[1]
    before = (jnp.arange(length)[:, None] > jnp.arange(length)[None, :]).astype(F32)
    counts = jnp.einsum("tu,pub->ptb", before, onehot, preferred_element_type=F32)
    rank = jnp.sum(onehot * counts, axis=2).astype(jnp.int32)
    return ids * slot_cap + rank


def layer_pages(rows_in, slots, live, grad_slots, weights):
    (wq, bq, wk, wv, bv, wo, bo, g1, s1, w1, b1, w2, b2, g2, s2) = weights
    pages, length, feat = rows_in.shape
    heads = feat // HEAD_DIM
    scale = HEAD_DIM**-0.5
    x_low = rows_in.reshape(-1, feat)
    select = (slots[:, None, :] == jnp.arange(grad_slots.shape[1])[None, :, None]).astype(BF16)
    grad_layer = jnp.einsum("pst,psd->ptd", select, grad_slots, preferred_element_type=F32)
    grad_layer = grad_layer.reshape(-1, feat)

    def split(flat):
        return flat.reshape(pages, length, heads, HEAD_DIM)

    query = split((dot(x_low, wq) + bq).astype(BF16))
    key = split(dot(x_low, wk).astype(BF16))
    value = split((dot(x_low, wv) + bv).astype(BF16))
    scores = jnp.einsum("pthd,puhd->phtu", query, key, preferred_element_type=F32) * scale
    scores = jnp.where(live[:, None, None, :], scores, NEG_FILL)
    shifted = jnp.exp(scores - jnp.max(scores, axis=-1, keepdims=True))
    probs = shifted / jnp.sum(shifted, axis=-1, keepdims=True)
    probs_low = probs.astype(BF16)
    mixed = jnp.einsum("phtu,puhd->pthd", probs_low, value, preferred_element_type=F32)
    attended = mixed.astype(BF16).reshape(-1, feat)
    normed_one, factor_one = norm_rows(x_low.astype(F32) + dot(attended, wo) + bo)
    hidden = normed_one * g1 + s1
    hidden_low = hidden.astype(BF16)
    inner = dot(hidden_low, w1) + b1
    cdf = 0.5 * (1.0 + lax.erf(inner * (0.5**0.5)))
    act_low = (inner * cdf).astype(BF16)
    slope = cdf + inner * jnp.exp(-0.5 * inner * inner) * ((0.5 / jnp.pi) ** 0.5)
    normed_two, factor_two = norm_rows(hidden + dot(act_low, w2) + b2)
    layer = (normed_two * g2 + s2).astype(BF16).reshape(pages, length, feat)
    layer_slots = jnp.einsum("pst,ptd->psd", select, layer, preferred_element_type=F32).astype(BF16)

    grad_g2 = jnp.sum(grad_layer * normed_two, axis=0)
    grad_s2 = jnp.sum(grad_layer, axis=0)
    grad_second = norm_back(grad_layer * g2, normed_two, factor_two)
    second_low = grad_second.astype(BF16)
    grad_w2 = dot_rows(act_low, second_low)
    grad_b2 = jnp.sum(second_low.astype(F32), axis=0)
    inner_low = (dot_cols(second_low, w2) * slope).astype(BF16)
    grad_w1 = dot_rows(hidden_low, inner_low)
    grad_b1 = jnp.sum(inner_low.astype(F32), axis=0)
    grad_hidden = grad_second + dot_cols(inner_low, w1)
    grad_g1 = jnp.sum(grad_hidden * normed_one, axis=0)
    grad_s1 = jnp.sum(grad_hidden, axis=0)
    grad_first = norm_back(grad_hidden * g1, normed_one, factor_one)
    first_low = grad_first.astype(BF16)
    grad_wo = dot_rows(attended, first_low)
    grad_bo = jnp.sum(first_low.astype(F32), axis=0)
    grad_att = split(dot_cols(first_low, wo).astype(BF16))
    grad_probs = jnp.einsum("pthd,puhd->phtu", grad_att, value, preferred_element_type=F32)
    inner_sum = jnp.sum(probs * grad_probs, axis=-1, keepdims=True)
    grad_scores = (probs * (grad_probs - inner_sum)).astype(BF16)

    def flat(per_head, factor):
        return (per_head * factor).astype(BF16).reshape(-1, feat)

    ein = lambda form, a, b: jnp.einsum(form, a, b, preferred_element_type=F32)
    grad_q = flat(ein("phtu,puhd->pthd", grad_scores, key), scale)
    grad_k = flat(ein("phtu,pthd->puhd", grad_scores, query), scale)
    grad_v = flat(ein("phtu,pthd->puhd", probs_low, grad_att), 1.0)
    grad_wq, grad_wk, grad_wv = (dot_rows(x_low, g) for g in (grad_q, grad_k, grad_v))
    grad_bq = jnp.sum(grad_q.astype(F32), axis=0)
    grad_bv = jnp.sum(grad_v.astype(F32), axis=0)
    grad_in = grad_first + dot_cols(grad_q, wq) + dot_cols(grad_k, wk) + dot_cols(grad_v, wv)
    grad_in = grad_in.astype(BF16).reshape(pages, length, feat)
    return (
        layer_slots,
        grad_in,
        (grad_wq, grad_bq, grad_wk, grad_wv, grad_bv, grad_wo, grad_bo, grad_g1, grad_s1)
        + (grad_w1, grad_b1, grad_w2, grad_b2, grad_g2, grad_s2),
    )


def to_pages(blocks):
    return lax.all_to_all(blocks, "band", split_axis=0, concat_axis=1, tiled=True)


def from_pages(blocks):
    return lax.all_to_all(blocks, "band", split_axis=1, concat_axis=0, tiled=True)


def split_ref(ref, which):
    rows, width = ref.shape[-2:]
    cut = width // 6
    if cut % 128:
        return ref.at[..., pl.ds(which * (rows // 2), rows // 2), :]
    return ref.at[..., pl.ds(which * cut, (cut, width - cut)[which])]


def split_shape(shape, which):
    rows, width = shape[-2:]
    cut = width // 6
    if cut % 128:
        return shape[:-2] + (rows // 2, width)
    return shape[:-1] + ((cut, width - cut)[which],)


def in_order(*calls):
    def step():
        for method, *index in calls:
            method(*index)

    return step


class Gather:
    def __init__(self, own, buf, sems, place):
        self.own, self.buf, self.place = own, buf, place
        self.zs, self.zr, self.ss, self.sr, self.fs, self.fr, self.cs, self.cr = sems

    def z_copy(self, j):
        z, x, y, c = self.place
        there = (z ^ (j + 1), x, y, c)
        return remote(self.own, self.buf.at[z, x, y, c], self.zs.at[j], self.zr.at[j], there)

    def side_copy(self, j, axis):
        z, x, y, c = self.place
        part = self.buf.at[z ^ j, x, y, c]
        there = (z, 1 - x, y, c) if axis == 0 else (z, x, 1 - y, c)
        source = self.own if j == 0 else part
        return remote(source, part, self.ss.at[axis, j], self.sr.at[axis, j], there)

    def far_copy(self, j, axis):
        z, x, y, c = self.place
        if axis == 0:
            part, there = self.buf.at[z ^ j, 1 - x, y, c], (z, x, 1 - y, c)
        else:
            part, there = self.buf.at[z ^ j, x, 1 - y, c], (z, 1 - x, y, c)
        part = split_ref(part, axis)
        return remote(part, part, self.fs.at[axis, j], self.fr.at[axis, j], there)

    def core_copy(self, k):
        z, x, y, c = self.place
        part = self.buf.at[:, (x, 1 - x, x, 1 - x)[k], (y, y, 1 - y, 1 - y)[k], c]
        return remote(part, part, self.cs.at[k], self.cr.at[k], (z, x, y, 1 - c))

    def start(self):
        for j in range(3):
            self.z_copy(j).start()
        for axis in (0, 1):
            self.side_copy(0, axis).start()

    def side(self, j):
        self.z_copy(j - 1).wait_recv()
        for axis in (0, 1):
            self.side_copy(j, axis).start()

    def far(self, j):
        for axis in (0, 1):
            self.side_copy(j, axis).wait_recv()
            self.far_copy(j, axis).start()

    def core(self, k):
        if k == 3:
            for j in range(4):
                for axis in (0, 1):
                    self.far_copy(j, axis).wait_recv()
        self.core_copy(k).start()

    def steps(self):
        side, far, core = self.side, self.far, self.core
        return [
            in_order((side, 1)),
            in_order((far, 0)),
            in_order((side, 2)),
            in_order((far, 1)),
            in_order((side, 3), (core, 0)),
            in_order((far, 2)),
            in_order((far, 3), (core, 1), (core, 2)),
            in_order((core, 3)),
        ]

    def arrive(self):
        for k in range(4):
            self.core_copy(k).wait_recv()

    def finish(self):
        for j in range(3):
            self.z_copy(j).wait_send()
        for j in range(4):
            for axis in (0, 1):
                self.side_copy(j, axis).wait_send()
                self.far_copy(j, axis).wait_send()
            self.core_copy(j).wait_send()


def gather_sems():
    return [DMA((3,)), DMA((3,))] + [DMA((2, 4))] * 4 + [DMA((4,))] * 2


def lanes(shape):
    return lax.broadcasted_iota(jnp.int32, shape, len(shape) - 1)


def rows_of(shape):
    return lax.broadcasted_iota(jnp.int32, shape, len(shape) - 2)


def columns(buf, start, width):
    return buf[:, :, :, :, :, pl.ds(start, width)].reshape(-1, width)


def unpack_rows(block, per_shard, width):
    shards, count, _ = block.shape
    spread = (rows_of((128, width)) == lanes((128, width)) % per_shard).astype(BF16)
    wide = dot(block.reshape(-1, 128), spread).reshape(shards, count, width)
    owner = lax.broadcasted_iota(jnp.int32, wide.shape, 0) == lanes(wide.shape) // per_shard
    return jnp.sum(jnp.where(owner, wide, 0.0), axis=0)


def pack_rows(rows, per_shard, shards):
    count, width = rows.shape
    wide = jnp.broadcast_to(rows[None], (shards, count, width))
    owner = lax.broadcasted_iota(jnp.int32, wide.shape, 0) == lanes(wide.shape) // per_shard
    wide = jnp.where(owner, wide, 0.0).astype(BF16).reshape(-1, width)
    spread = (lanes((width, 128)) == rows_of((width, 128)) % per_shard).astype(BF16)
    return dot(wide, spread).astype(BF16).reshape(shards, count, 128)


def block_of(i, size):
    return pl.ds(pl.multiple_of(i * size, size), size)


def gelu_parts(v):
    cdf = 0.5 * (1.0 + lax.erf(v * (0.5**0.5)))
    return v * cdf, cdf + v * jnp.exp(-0.5 * v * v) * ((0.5 / jnp.pi) ** 0.5)


class Out:
    def __init__(self, sems):
        self.sems, self.copies = sems, []

    def send(self, src, dst):
        copy = pltpu.make_async_copy(src, dst, self.sems.at[len(self.copies)])
        copy.start()
        self.copies.append(copy)

    def wait(self):
        for copy in self.copies:
            copy.wait()


BIAS_ROWS = 8
TILE = 256


def forward_kernel(
    tokens, grads, live, slots, w_q, w_k, w_v, w_o, w_1, w_2, small_in,
    qkv_out, lse, x_out, att_out, normed1_out, low_out, act_out, slope_out, normed2_out,
    factors, bias, q_out, k_out, v_out, o_out, w1_out, w2_out, grad_pages, layer_slots,
    small, a_buf, w1_buf, w2_buf, x_buf, qkv, att, normed1, low, act, slope, second, normed2, layer, bias1,
    local, ts, tr, gs, gr, outs, *sems,
):
    place = z, x, y, c = my_place()
    me = y * 2 + c
    length, feat = low.shape
    pairs = feat // 128
    x_rows = x_buf.reshape(length, feat)
    here = (z, x, y, c)
    copies = [
        pltpu.make_async_copy(src, dst, local.at[i])
        for i, (src, dst) in enumerate(
            [(w, a_buf.at[here + (slice(None), pl.ds(i * feat, feat))]) for i, w in enumerate((w_q, w_k, w_v, w_o))]
            + [(small_in, small.at[here]), (w_1, w1_buf.at[here]), (w_2, w2_buf.at[here])]
            + [(tokens.at[me], x_buf.at[me]), (grads.at[me], grad_pages.at[me])]
        )
    ]
    for copy in copies:
        copy.start()
    meet(
        [(z ^ j, x, y, c) for j in (1, 2, 3)]
        + [(z, 1 - x, y, c), (z, x, 1 - y, c), (z, x, y, 1 - c), (z, x, 1 - y, 1 - c)]
    )

    def page_copy(src, dst, send, recv, j):
        there = me ^ (j + 1)
        return remote(src.at[there], dst.at[me], send.at[j], recv.at[j], (z, x, there // 2, there % 2))

    token_copies = [page_copy(tokens, x_buf, ts, tr, j) for j in range(3)]
    grad_copies = [page_copy(grads, grad_pages, gs, gr, j) for j in range(3)]
    gathers = [
        Gather(own, buf, sems[8 * i : 8 * i + 8], place)
        for i, (own, buf) in enumerate(
            [(small_in, small), (a_buf.at[here], a_buf), (w_1, w1_buf), (w_2, w2_buf)]
        )
    ]
    vectors, atts, inner, outer = gathers
    for copy in copies[:5]:
        copy.wait()
    atts.start()
    vectors.start()
    for copy in token_copies:
        copy.start()
    later_1, later_2 = inner.steps(), outer.steps()
    for i, (first, other) in enumerate(zip(vectors.steps(), atts.steps())):
        other()
        first()
        if i == 2:
            inner.start()
        if i == 5:
            outer.start()
        if i == 6:
            later_1[0]()
    for copy in copies[5:]:
        copy.wait()
    for copy in grad_copies:
        copy.start()
    vectors.arrive()
    shards = small[...].reshape(32, 16, 128)
    bias[...] = unpack_rows(shards[:, :8], feat // 32, feat)
    inner_width = act.shape[1]
    for i in range(4):
        part = unpack_rows(small[i].reshape(8, 16, 128)[:, 8:], inner_width // 32, inner_width // 4)
        bias1[:, i * (inner_width // 4) : (i + 1) * (inner_width // 4)] = part
    for copy in token_copies:
        copy.wait_recv()
    atts.arrive()
    out = Out(outs)
    for i, ref in enumerate((q_out, k_out, v_out, o_out)):
        out.send(a_buf.at[:, :, :, :, :, pl.ds(i * feat, feat)], ref)
    out.send(x_rows, x_out)
    for step in later_1[1:3]:
        step()

    def project(j, _):
        start = pl.multiple_of(j * TILE, TILE)
        total = dot(x_rows[...], columns(a_buf, start, TILE))
        which = j // (feat // TILE)
        inside = block_of(j % (feat // TILE), TILE)
        row = jnp.where(which == 0, bias[0:1, inside], jnp.where(which == 2, bias[1:2, inside], 0.0))
        qkv[:, pl.ds(start, TILE)] = (total + row).astype(BF16)
        return 0

    lax.fori_loop(0, 3 * feat // TILE, project, 0)
    out.send(qkv, qkv_out)
    for step in later_1[3:5]:
        step()
    under = [
        [later_1[5], later_2[0]],
        [later_1[6], later_2[1], later_2[2]],
        [later_1[7], later_2[3]],
        [later_2[4]],
        [later_2[5]],
        [later_2[6]],
    ]
    scale = HEAD_DIM**-0.5

    def pair(p, _):
        start = pl.multiple_of(p * 128, 128)
        q = qkv[:, pl.ds(start, 128)] * jnp.asarray(scale, BF16)
        k = qkv[:, pl.ds(feat + start, 128)]
        v = qkv[:, pl.ds(2 * feat + start, 128)]
        low_lane = lanes(q.shape) < HEAD_DIM
        mixed = []
        for h in (0, 1):
            part = jnp.where(low_lane if h == 0 else ~low_lane, k, jnp.zeros_like(k))
            scores = jnp.where(live[...] > 0, dot_cols(part, q), NEG_FILL)
            top = jnp.max(scores, axis=0, keepdims=True)
            shifted = jnp.exp(scores - top)
            total = jnp.sum(shifted, axis=0, keepdims=True)
            probs = (shifted * (1.0 / total)).astype(BF16)
            mixed.append(dot_rows(v, probs))
            lse[pl.ds(2 * p + h, 1), :] = top + jnp.log(total)
        both = jnp.where(rows_of(mixed[0].shape) < HEAD_DIM, mixed[0], mixed[1])
        att[:, pl.ds(start, 128)] = both.T.astype(BF16)
        for i, steps in enumerate(under):
            pl.when(p == i)(in_order(*[(step,) for step in steps]))
        return 0

    lax.fori_loop(0, pairs, pair, 0)
    out.send(att, att_out)
    rows = 128

    def norm_one(i, _):
        block = block_of(i, rows)
        total = dot(att[block, :], columns(a_buf, 3 * feat, feat))
        total = total + x_rows[block, :].astype(F32) + bias[2:3, :]
        normed, factor = norm_rows(total)
        normed1[block, :] = normed
        factors[block, 0:128] = jnp.broadcast_to(factor, (rows, 128))
        low[block, :] = (normed * bias[3:4, :] + bias[4:5, :]).astype(BF16)
        return 0

    lax.fori_loop(0, length // rows, norm_one, 0)
    out.send(normed1, normed1_out)
    out.send(low, low_out)
    inner.arrive()
    out.send(w1_buf, w1_out)
    later_2[7]()

    def ffn_in(j, _):
        block = block_of(j, TILE)
        value, grad = gelu_parts(dot(low[...], columns(w1_buf, block.start, TILE)) + bias1[0:1, block])
        act[:, block] = value.astype(BF16)
        slope[:, block] = grad.astype(BF16)
        return 0

    lax.fori_loop(0, inner_width // TILE, ffn_in, 0)
    out.send(act, act_out)
    out.send(slope, slope_out)
    outer.arrive()
    out.send(w2_buf, w2_out)

    def ffn_out(j, _):
        block = block_of(j, TILE)
        second[:, block] = dot(act[...], columns(w2_buf, block.start, TILE))
        return 0

    lax.fori_loop(0, feat // TILE, ffn_out, 0)

    def norm_two(i, _):
        block = block_of(i, rows)
        hidden = normed1[block, :] * bias[3:4, :] + bias[4:5, :]
        normed, factor = norm_rows(hidden + second[block, :] + bias[5:6, :])
        normed2[block, :] = normed
        factors[block, 128:256] = jnp.broadcast_to(factor, (rows, 128))
        layer[block, :] = (normed * bias[6:7, :] + bias[7:8, :]).astype(BF16)
        return 0

    lax.fori_loop(0, length // rows, norm_two, 0)
    out.send(normed2, normed2_out)

    def place_rows(i, _):
        cap = layer_slots.shape[1]
        here_rows = rows_of((cap, length)) + i * cap
        select = (here_rows == slots[...]).astype(BF16)
        layer_slots[i] = dot(select, layer[...]).astype(BF16)
        return 0

    lax.fori_loop(0, layer_slots.shape[0], place_rows, 0)
    for copy in grad_copies:
        copy.wait_recv()
    for copy in grad_copies + token_copies:
        copy.wait_send()
    for one in gathers:
        one.finish()
    out.wait()


def forward(tokens, grads, live, slots, w_q, w_k, w_v, w_o, w_1, w_2, small):
    length, feat, inner_width = slots.shape[1], tokens.shape[-1], w_1.shape[1]
    anywhere = pl.BlockSpec(memory_space=pl.ANY)
    vmem = pl.BlockSpec(memory_space=pltpu.VMEM)
    grid = (4, 2, 2, 2)
    heads = feat // HEAD_DIM
    results = [
        ((length, 3 * feat), BF16, anywhere),
        ((heads + -heads % 8, length), F32, vmem),
        ((length, feat), BF16, anywhere),
        ((length, feat), BF16, anywhere),
        ((length, feat), F32, anywhere),
        ((length, feat), BF16, anywhere),
        ((length, inner_width), BF16, anywhere),
        ((length, inner_width), BF16, anywhere),
        ((length, feat), F32, anywhere),
        ((length, 256), F32, vmem),
        ((BIAS_ROWS, feat), F32, vmem),
    ]
    results += [(grid + w_q.shape, BF16, anywhere)] * 4
    results += [(grid + w_1.shape, BF16, anywhere), (grid + w_2.shape, BF16, anywhere)]
    results += [(grads.shape, BF16, anywhere), (grads.shape, BF16, vmem)]
    return pl.pallas_call(
        forward_kernel,
        out_shape=[jax.ShapeDtypeStruct(shape, kind) for shape, kind, _ in results],
        in_specs=[anywhere, anywhere, vmem, vmem] + [anywhere] * 7,
        out_specs=[spec for _, _, spec in results],
        scratch_shapes=[
            pltpu.VMEM(grid + small.shape, BF16),
            pltpu.VMEM(grid + (w_q.shape[0], 4 * feat), BF16),
            pltpu.VMEM(grid + w_1.shape, BF16),
            pltpu.VMEM(grid + w_2.shape, BF16),
            pltpu.VMEM(tokens.shape, BF16),
            pltpu.VMEM((length, 3 * feat), BF16),
            pltpu.VMEM((length, feat), BF16),
            pltpu.VMEM((length, feat), F32),
            pltpu.VMEM((length, feat), BF16),
            pltpu.VMEM((length, inner_width), BF16),
            pltpu.VMEM((length, inner_width), BF16),
            pltpu.VMEM((length, feat), F32),
            pltpu.VMEM((length, feat), F32),
            pltpu.VMEM((length, feat), BF16),
            pltpu.VMEM((8, inner_width), F32),
            DMA((9,)),
            DMA((3,)),
            DMA((3,)),
            DMA((3,)),
            DMA((3,)),
            DMA((14,)),
        ]
        + gather_sems() * 4,
        compiler_params=pltpu.CompilerParams(
            collective_id=0, has_side_effects=True, vmem_limit_bytes=VMEM_LIMIT
        ),
        name="forward",
    )(tokens, grads, live, slots, w_q, w_k, w_v, w_o, w_1, w_2, small)


def add_into(dst, src, lead):
    def step(flat, _):
        index = []
        for size in reversed(lead):
            index.append(flat % size)
            flat = flat // size
        index = tuple(reversed(index))
        dst[index] = (dst[index].astype(F32) + src[index].astype(F32)).astype(BF16)
        return 0

    total = 1
    for size in lead:
        total *= size
    lax.fori_loop(0, total, step, 0)


class Reduce:
    def __init__(self, part, bufs, sems, place, write, by_z):
        self.part, self.place, self.write = part, place, write
        self.got_core, self.got_1, self.got_2, self.got_z = bufs[0], bufs[1:3], bufs[3:5], bufs[5]
        self.cs, self.cr, self.fs, self.fr, self.ss, self.sr, self.zs, self.zr = sems
        self.chunks = (3, 2, 1, 0) if by_z else (0,)
        self.by_z = by_z

    def at(self, j):
        return self.place[0] ^ j if self.by_z else slice(None)

    def lead(self, *rest):
        return rest if self.by_z else (4,) + rest

    def core_copy(self, j):
        z, x, y, c = self.place
        zi = self.at(j)
        there = (z, x, y, 1 - c)
        return remote(self.part.at[zi, :, :, 1 - c], self.got_core.at[zi], self.cs.at[j], self.cr.at[j], there)

    def first_copy(self, j, axis):
        z, x, y, c = self.place
        zi = self.at(j)
        if axis == 0:
            part, there = self.part.at[zi, :, 1 - y, c], (z, x, 1 - y, c)
        else:
            part, there = self.part.at[zi, 1 - x, :, c], (z, 1 - x, y, c)
        return remote(split_ref(part, axis), self.got_1[axis].at[zi], self.fs.at[axis, j], self.fr.at[axis, j], there)

    def second_copy(self, j, axis):
        z, x, y, c = self.place
        zi = self.at(j)
        if axis == 0:
            part, there = self.part.at[zi, 1 - x, y, c], (z, 1 - x, y, c)
        else:
            part, there = self.part.at[zi, x, 1 - y, c], (z, x, 1 - y, c)
        return remote(split_ref(part, axis), self.got_2[axis].at[zi], self.ss.at[axis, j], self.sr.at[axis, j], there)

    def z_copy(self, j):
        z, x, y, c = self.place
        part = self.part.at[z ^ j, x, y, c]
        return remote(part, self.got_z.at[j - 1], self.zs.at[j - 1], self.zr.at[j - 1], (z ^ j, x, y, c))

    def send(self, j):
        self.core_copy(j).start()

    def send_all(self):
        for j in self.chunks:
            self.send(j)

    def first(self, j):
        z, x, y, c = self.place
        zi = self.at(j)
        self.core_copy(j).wait_recv()
        add_into(self.part.at[zi, :, :, c], self.got_core.at[zi], self.lead(2, 2))
        for axis in (0, 1):
            self.first_copy(j, axis).start()

    def second(self, j):
        z, x, y, c = self.place
        zi = self.at(j)
        for axis in (0, 1):
            self.first_copy(j, axis).wait_recv()
            part = self.part.at[zi, :, y, c] if axis == 0 else self.part.at[zi, x, :, c]
            add_into(split_ref(part, axis), self.got_1[axis].at[zi], self.lead(2))
            self.second_copy(j, axis).start()

    def along_z(self, j):
        z, x, y, c = self.place
        zi = self.at(j)
        for axis in (0, 1):
            self.second_copy(j, axis).wait_recv()
            part = split_ref(self.part.at[zi, x, y, c], axis)
            got = self.got_2[axis].at[zi]
            if self.by_z:
                part[...] = (part[...].astype(F32) + got[...].astype(F32)).astype(BF16)
            else:
                add_into(part, got, (4,))
        for i in (1, 2, 3):
            if not self.by_z or i == j:
                self.z_copy(i).start()

    def last(self):
        z, x, y, c = self.place
        total = self.part[z, x, y, c].astype(F32)
        for i in (1, 2, 3):
            self.z_copy(i).wait_recv()
            total = total + self.got_z[i - 1].astype(F32)
        self.write(total)

    def steps(self):
        first, second, along = self.first, self.second, self.along_z
        if not self.by_z:
            return [in_order((first, 0)), in_order((second, 0)), in_order((along, 0)), in_order((self.last,))]
        return [
            in_order((first, 3)),
            in_order((first, 2), (second, 3)),
            in_order((first, 1), (second, 2), (along, 3)),
            in_order((first, 0), (second, 1), (along, 2)),
            in_order((second, 0), (along, 1)),
            in_order((along, 0)),
            in_order((self.last,)),
        ]

    def finish(self):
        for j in self.chunks:
            self.core_copy(j).wait_send()
            for axis in (0, 1):
                self.first_copy(j, axis).wait_send()
                self.second_copy(j, axis).wait_send()
        for i in (1, 2, 3):
            self.z_copy(i).wait_send()


def reduce_sems():
    return [DMA((4,))] * 2 + [DMA((2, 4))] * 4 + [DMA((3,))] * 2


def reduce_bufs(rows, width):
    shape = (rows, width)
    return [
        pltpu.VMEM((4, 2, 2) + shape, BF16),
        pltpu.VMEM(split_shape((4, 2) + shape, 0), BF16),
        pltpu.VMEM(split_shape((4, 2) + shape, 1), BF16),
        pltpu.VMEM(split_shape((4,) + shape, 0), BF16),
        pltpu.VMEM(split_shape((4,) + shape, 1), BF16),
        pltpu.VMEM((3,) + shape, BF16),
    ]


PIECES = 7
GROUPS = 3


def backward_kernel(
    qkv_in, lse, x_in, att_in, normed1_in, low_in, act_in, slope_in, normed2_in, factors, bias,
    w_q, w_k, w_v, w_o, w1_in, w2_in, grads_in, layer_in, slots, live,
    layer_out, tokens_out, q_out, k_out, v_out, o_out, w1_out, w2_out, small_out,
    qkv, x, att, normed1, low, act, slope, grad, grads, w1, wb, turned, d_qkv, g_2, g_1, g_o, g_qkv, g_small, sums, sums1,
    local, ls, lr, ts, tr, *rest,
):
    place = z, px, py, c = my_place()
    me = py * 2 + c
    length, feat = low.shape
    inner_width = act.shape[1]
    bufs, sems = rest[: 6 * PIECES], rest[6 * PIECES :]
    slots_each = grads.shape[0] // 4

    sources = [(grads_in.at[i], grads.at[pl.ds(i * slots_each, slots_each)]) for i in range(4)]
    sources += [(normed2_in, grad), (act_in, act), (w2_in, wb), (slope_in, slope), (low_in, low), (w1_in, w1)]
    sources += [(normed1_in, normed1), (att_in, att), (qkv_in, qkv), (x_in, x)]
    loads = [pltpu.make_async_copy(src, dst, local.at[i]) for i, (src, dst) in enumerate(sources)]
    for copy in loads:
        copy.start()
    meet(
        [(z ^ j, px, py, c) for j in (1, 2, 3)]
        + [(z, 1 - px, py, c), (z, px, 1 - py, c), (z, px, py, 1 - c), (z, px, 1 - py, 1 - c)]
    )

    def page_copy(src, dst, send, recv, j):
        there = me ^ (j + 1)
        return remote(src.at[there], dst.at[me], send.at[j], recv.at[j], (z, px, there // 2, there % 2))

    layer_copies = [page_copy(layer_in, layer_out, ls, lr, j) for j in range(3)]
    for copy in layer_copies:
        copy.start()
    layer_own = pltpu.make_async_copy(layer_in.at[me], layer_out.at[me], local.at[14])
    layer_own.start()

    def whole(ref):
        def write(total):
            ref[...] = total

        return write

    def thirds(group):
        def write(total):
            for i, ref in enumerate((q_out, k_out, v_out)):
                ref[:, pl.ds(group * TILE, TILE)] = total[:, i * TILE : (i + 1) * TILE]

        return write

    parts = [(g_2, whole(w2_out), True), (g_1, whole(w1_out), True), (g_o, whole(o_out), False)]
    parts += [(g_qkv.at[i], thirds(i), False) for i in range(GROUPS)]
    parts += [(g_small, whole(small_out), False)]
    sums_2, sum_1, sum_o, *sum_qkv, sum_small = reduces = [
        Reduce(part, bufs[6 * i : 6 * i + 6], sems[8 * i : 8 * i + 8], place, write, by_z)
        for i, (part, write, by_z) in enumerate(parts)
    ]
    steps_2, steps_1, steps_o, *steps_qkv, steps_small = [one.steps() for one in reduces]

    sums[...] = jnp.zeros_like(sums)
    sums1[...] = jnp.zeros_like(sums1)

    def tally(row, values):
        sums[row : row + 1, :] += jnp.sum(values, axis=0, keepdims=True)

    for copy in loads[:5]:
        copy.wait()
    rows = 128

    def norm_two(i, _):
        block = block_of(i, rows)
        select = (rows_of((grads.shape[0], rows)) == slots[:, block]).astype(BF16)
        grad_layer = dot_rows(select, grads[...])
        normed = grad[block, :]
        tally(6, grad_layer * normed)
        tally(7, grad_layer)
        back = norm_back(grad_layer * bias[6:7, :], normed, factors[block, 128:129])
        grad[block, :] = back
        second_low = back.astype(BF16)
        d_qkv[block, 0:feat] = second_low
        tally(5, second_low.astype(F32))
        return 0

    lax.fori_loop(0, length // rows, norm_two, 0)
    second = grads.at[pl.ds(0, length)]
    second[...] = d_qkv[:, 0:feat]
    loads[5].wait()

    def outer_grad(i, _):
        j = 3 - i
        zi = z ^ j
        width = inner_width // 4
        part = dot_rows(act[:, block_of(zi, width)], second[...])
        g_2[zi] = part.astype(BF16).reshape(g_2.shape[1:])
        sums_2.send(j)
        return 0

    lax.fori_loop(0, 4, outer_grad, 0)
    for copy in loads[6:9]:
        copy.wait()
    turned[...] = low[...].T
    when_2 = {2: 0, 4: 1, 6: 2, 8: 3, 10: 4}

    def inner_grad(i, _):
        block = block_of(i, TILE)
        up = dot_cols(second[...], wb[block, :])
        inner_low = (up * slope[:, block].astype(F32)).astype(BF16)
        slope[:, block] = inner_low
        sums1[0:1, block] = jnp.sum(inner_low.astype(F32), axis=0, keepdims=True)
        part = dot(turned[...], inner_low)
        g_1[:, :, :, :, :, block] = part.astype(BF16).reshape(g_1.shape[:-1] + (TILE,))
        for at, index in when_2.items():
            pl.when(i == at)(steps_2[index])
        return 0

    lax.fori_loop(0, inner_width // TILE, inner_grad, 0)
    sum_1.send_all()
    slabs = [
        pltpu.make_async_copy(src, wb.at[pl.ds(i * feat, feat)], local.at[15 + i])
        for i, src in enumerate((w_o, w_q, w_k, w_v))
    ]
    for copy in slabs:
        copy.start()
    for copy in loads[9:]:
        copy.wait()
    steps_2[5]()

    def hidden_grad(i, _):
        half_width = feat // 2
        block = block_of(i, half_width)
        weight = w1[pl.ds(2 * i, 2)].reshape(half_width, inner_width)
        grad[:, block] += dot_cols(slope[...], weight)
        return 0

    lax.fori_loop(0, 2, hidden_grad, 0)
    steps_1[0]()
    first = second

    def norm_one(i, _):
        block = block_of(i, rows)
        up, normed = grad[block, :], normed1[block, :]
        tally(3, up * normed)
        tally(4, up)
        back = norm_back(up * bias[3:4, :], normed, factors[block, 0:1])
        grad[block, :] = back
        first_low = back.astype(BF16)
        first[block, :] = first_low
        tally(2, first_low.astype(F32))
        return 0

    lax.fori_loop(0, length // rows, norm_one, 0)
    for copy in slabs:
        copy.wait()
    g_o[...] = dot_rows(att[...], first[...]).astype(BF16).reshape(g_o.shape)
    sum_o.send_all()
    grad_att = grads.at[pl.ds(length, length)]

    def att_grad(i, _):
        block = block_of(i, rows)
        grad_att[block, :] = dot_cols(first[block, :], wb[0:feat, :]).astype(BF16)
        return 0

    lax.fori_loop(0, length // rows, att_grad, 0)
    turned[...] = x[...].T
    steps_1[1]()
    scale = HEAD_DIM**-0.5

    def pair(p):
        start = pl.multiple_of(p * 128, 128)
        q = qkv[:, pl.ds(start, 128)] * jnp.asarray(scale, BF16)
        k = qkv[:, pl.ds(feat + start, 128)]
        v = qkv[:, pl.ds(2 * feat + start, 128)]
        g = grad_att[:, pl.ds(start, 128)]
        low_lane = lanes(q.shape) < HEAD_DIM
        results = []
        for h in (0, 1):
            keep = low_lane if h == 0 else ~low_lane
            zero = jnp.zeros_like(k)
            scores = jnp.where(live[...] > 0, dot_cols(jnp.where(keep, k, zero), q), NEG_FILL)
            probs = jnp.exp(scores - lse[pl.ds(2 * p + h, 1), :])
            up = dot_cols(jnp.where(keep, v, zero), g)
            inner_sum = jnp.sum(probs * up, axis=0, keepdims=True)
            grad_scores = (probs * (up - inner_sum)).astype(BF16)
            results.append((dot_rows(k, grad_scores), dot(grad_scores, q), dot(probs.astype(BF16), g)))
        (q_0, k_0, v_0), (q_1, k_1, v_1) = results
        d_q = jnp.where(rows_of(q_0.shape) < HEAD_DIM, q_0, q_1) * scale
        d_qkv[:, pl.ds(start, 128)] = d_q.T.astype(BF16)
        d_qkv[:, pl.ds(feat + start, 128)] = jnp.where(low_lane, k_0, k_1).astype(BF16)
        d_qkv[:, pl.ds(2 * feat + start, 128)] = jnp.where(low_lane, v_0, v_1).astype(BF16)

    under = [
        [steps_1[2], steps_2[6]],
        [steps_1[3], steps_o[0]],
        [steps_1[4], steps_o[1]],
        [steps_1[5], steps_qkv[0][0]],
        [steps_o[2], steps_qkv[0][1]],
        [steps_1[6], steps_qkv[1][0]],
    ]

    def group(i, _):
        def one(j, _):
            p = 2 * i + j
            pair(p)
            for at, steps in enumerate(under):
                pl.when(p == at)(in_order(*[(step,) for step in steps]))
            return 0

        lax.fori_loop(0, 2, one, 0)
        for t in range(3):
            cols = pl.ds(pl.multiple_of(t * feat + i * TILE, TILE), TILE)
            part = dot(turned[...], d_qkv[:, cols])
            g_qkv[i, :, :, :, :, :, pl.ds(t * TILE, TILE)] = part.astype(BF16).reshape(
                g_qkv.shape[1:-1] + (TILE,)
            )
        for at in range(GROUPS):
            pl.when(i == at)(sum_qkv[at].send_all)
        return 0

    lax.fori_loop(0, GROUPS, group, 0)
    tally(0, d_qkv[:, 0:feat].astype(F32))
    tally(1, d_qkv[:, 2 * feat : 3 * feat].astype(F32))
    g_small[:, :, :, :, 0:8, :] = pack_rows(sums[...], feat // 32, 32).reshape(4, 2, 2, 2, 8, 128)
    for i in range(4):
        part = sums1[:, i * (inner_width // 4) : (i + 1) * (inner_width // 4)]
        g_small[i, :, :, :, 8:16, :] = pack_rows(part, inner_width // 32, 8).reshape(2, 2, 2, 8, 128)
    sum_small.send_all()
    steps_qkv[2][0]()

    def token_grad(i, _):
        block = block_of(i, rows)
        total = grad[block, :]
        for t in range(3):
            total += dot_cols(
                d_qkv[block, t * feat : (t + 1) * feat], wb[(t + 1) * feat : (t + 2) * feat, :]
            )
        x[block, :] = total.astype(BF16)
        return 0

    lax.fori_loop(0, length // rows, token_grad, 0)
    grad_tokens = x.reshape(4, length // 4, feat)
    token_copies = [page_copy(grad_tokens, tokens_out, ts, tr, j) for j in range(3)]
    for copy in token_copies:
        copy.start()
    token_own = pltpu.make_async_copy(grad_tokens.at[me], tokens_out.at[me], local.at[19])
    token_own.start()
    steps_small[0]()
    steps_qkv[1][1]()
    steps_o[3]()
    steps_qkv[0][2]()
    steps_qkv[2][1]()
    steps_small[1]()
    steps_qkv[1][2]()
    steps_qkv[0][3]()
    steps_qkv[2][2]()
    steps_small[2]()
    steps_qkv[1][3]()
    steps_qkv[2][3]()
    steps_small[3]()
    for copy in layer_copies + token_copies:
        copy.wait()
    layer_own.wait()
    token_own.wait()
    for one in reduces:
        one.finish()


def backward(saved, weights, grad_pages, layer_slots, slots, live, tokens_shape):
    w_q, w_1, w_2 = weights[0], weights[4], weights[5]
    qkv, lse, x, att, normed1, low, act, slope, normed2, factors, bias = saved
    length, feat = low.shape
    inner_width = act.shape[1]
    anywhere = pl.BlockSpec(memory_space=pl.ANY)
    vmem = pl.BlockSpec(memory_space=pltpu.VMEM)
    grid = (4, 2, 2, 2)
    small, inner, outer = (feat // 32, feat), (feat // 32, inner_width), (inner_width // 32, feat)
    sizes = [outer, inner] + [small] * 4 + [(16, 128)]
    scratch = [
        ((length, 3 * feat), BF16),
        ((length, feat), BF16),
        ((length, feat), BF16),
        ((length, feat), F32),
        ((length, feat), BF16),
        ((length, inner_width), BF16),
        ((length, inner_width), BF16),
        ((length, feat), F32),
        ((grad_pages.shape[0] * grad_pages.shape[1], feat), BF16),
        (grid + inner, BF16),
        ((inner_width, feat), BF16),
        ((feat, length), BF16),
        ((length, 3 * feat), BF16),
        (grid + outer, BF16),
        (grid + inner, BF16),
        (grid + small, BF16),
        ((GROUPS,) + grid + small, BF16),
        (grid + (16, 128), BF16),
        ((8, feat), F32),
        ((8, inner_width), F32),
    ]
    bufs, sems = [], []
    for size in sizes:
        bufs += reduce_bufs(*size)
        sems += reduce_sems()
    outs = [(grad_pages.shape, BF16, anywhere), (tokens_shape, BF16, anywhere)]
    outs += [(small, F32, vmem)] * 4 + [(inner, F32, vmem), (outer, F32, vmem), ((16, 128), F32, vmem)]
    return pl.pallas_call(
        backward_kernel,
        out_shape=[jax.ShapeDtypeStruct(shape, kind) for shape, kind, _ in outs],
        in_specs=[anywhere, vmem] + [anywhere] * 7 + [vmem, vmem] + [anywhere] * 8 + [vmem, vmem],
        out_specs=[spec for _, _, spec in outs],
        scratch_shapes=[pltpu.VMEM(shape, kind) for shape, kind in scratch]
        + [DMA((20,)), DMA((3,)), DMA((3,)), DMA((3,)), DMA((3,))]
        + bufs
        + sems,
        compiler_params=pltpu.CompilerParams(
            collective_id=1, has_side_effects=True, vmem_limit_bytes=VMEM_LIMIT
        ),
        name="backward",
    )(*saved, *weights, grad_pages, layer_slots, slots, live)


def small_shard(weights):
    rows = [jnp.pad(weights[i], (0, 128 - weights[i].shape[0])) for i in SMALL_ORDER]
    rows += [jnp.zeros_like(rows[0])] * (16 - len(rows))
    return jnp.stack(rows)


SMALL_ORDER = (1, 4, 6, 7, 8, 12, 13, 14, 10)


def by_kernels(tokens, band_ids, page_mask, weights, grad_output):
    bands = lax.axis_size("band")
    me = lax.axis_index("band")
    slot_cap, feat = grad_output.shape[1:]
    ids = lax.dynamic_slice_in_dim(band_ids, me, 1, 0)
    live = lax.dynamic_slice_in_dim(page_mask, me, 1, 0)
    slots = page_slots(ids, bands, slot_cap)
    large = [weights[i] for i in (0, 2, 3, 5, 9, 11)]
    got = forward(tokens, grad_output, live.reshape(-1, 1), slots, *large, small_shard(weights))
    saved, full, grad_slots, layer_slots = got[:11], got[11:17], got[17], got[18]
    full = [w if i == 4 else w.reshape(-1, w.shape[-1]) for i, w in enumerate(full)]
    sums = backward(saved, full, grad_slots, layer_slots, slots, live.reshape(-1, 1), tokens.shape)
    grads = [None] * len(weights)
    for i, total in zip((0, 2, 3, 5, 9, 11), sums[2:8]):
        grads[i] = total
    for row, i in enumerate(SMALL_ORDER):
        grads[i] = sums[8][row, : weights[i].shape[0]]
    return tuple(sums[:2]) + tuple(grads)


def per_device(hand_made, *args):
    tokens, band_ids, band_counts, page_mask = args[:4]
    weights, grad_output = args[4:19], args[19]
    if hand_made:
        return by_kernels(tokens, band_ids, page_mask, weights, grad_output)
    bands = lax.axis_size("band")
    slot_cap = grad_output.shape[1]
    pages = tokens.shape[0] // bands
    full = [lax.all_gather(w, BOTH, axis=0, tiled=True) for w in weights]
    first = lax.axis_index("band") * pages
    ids = lax.dynamic_slice_in_dim(band_ids, first, pages, 0)
    live = lax.dynamic_slice_in_dim(page_mask, first, pages, 0) > 0
    slots = page_slots(ids, bands, slot_cap)
    layer_slots, grad_in, grads = layer_pages(
        to_pages(tokens), slots, live, to_pages(grad_output), full
    )
    return (from_pages(layer_slots), from_pages(grad_in)) + tuple(
        lax.psum_scatter(g, BOTH, scatter_dimension=0, tiled=True) for g in grads
    )


def solution(mesh):
    hand_made = dict(mesh.shape) == {"page": 8, "band": 4}
    shard = P(BOTH)
    rows = P(BOTH, None)
    tokens = P("page", "band", None)
    page = P("page", None)
    weights = (rows, shard, rows, rows, shard, rows, shard, shard, shard)
    weights = weights + (rows, shard, rows, shard, shard, shard)

    def step(*args):
        return per_device(hand_made, *args)

    return jax.shard_map(
        step,
        mesh=mesh,
        in_specs=(tokens, page, page, page) + weights + (tokens,),
        out_specs=(tokens, tokens) + weights,
        check_vma=False,
    )
```

profile of v0, /device:TPU:0, one launch (start us, length us, event | category | flops | bytes accessed | tf_op | source)
XLA Modules:
  0.0 242.3 jit_solution(18335635546396146941)
XLA Ops:
  0.7 0.7 pad_bitcast_fusion.8
  1.3 0.7 pad_bitcast_fusion.6
  2.0 0.7 pad_bitcast_fusion.4
  2.7 0.7 pad_bitcast_fusion
  3.3 0.7 pad_bitcast_fusion.2
  4.0 1.2 stack.47.small_in
  5.3 0.7 dynamic-slice_bitcast_fusion
  6.0 0.4 fusion.1
  6.4 0.6 multiply_add_fusion.slots
  7.0 0.9 copy.36.live
  7.8 107.1 %forward.1 = (bf16[512,2304]{1,0:T(8,128)(2,1)}, f32[16,512]{1,0:T(8,128)}, bf16[512,768]{1,0:T(8,128)(2,1)}, bf16[512,768]{1,0:T(8,128)(2,1)}, f32[512,768]{1,0...) custom-call(bf16[4,128,768]{2,1,0:T(8,128)(2,1)} %tokens.1, ...), custom_call_target="tpu_custom_call" | custom-call | tf_op jit(solution)/shard_map/forward/pallas_call | solution.py:559
  114.9 117.1 %backward.1 = (bf16[4,256,768]{2,1,0:T(8,128)(2,1)}, bf16[4,128,768]{2,1,0:T(8,128)(2,1)}, f32[24,768]{1,0:T(8,128)}, f32[24,768]{1,0:T(8,128)}, f32[24,768]{1,0...) custom-call(bf16[512,2304]{1,0:T(8,128)(2,1)} %get-tuple-element.45.qkv_in, ...), custom_call_target="tpu_custom_call" | custom-call | tf_op jit(solution)/shard_map/backward/pallas_call | solution.py:1047
  232.0 1.2 slice_bitcast_fusion.3
  233.2 1.5 slice_bitcast_fusion
  234.7 0.0 copy-start
  234.7 2.7 %copy.46 = bf16[4,256,768]{2,1,0:T(8,128)(2,1)} copy(bf16[4,256,768]{2,1,0:T(8,128)(2,1)} %get-tuple-element.108) | data formatting | bytes 3145728
  237.4 0.0 copy-done
  237.4 0.0 copy-start.6
  237.4 0.0 copy-start.5
  237.4 0.0 copy-start.4
  237.5 0.0 copy-start.3
  237.5 0.0 copy-start.2
  237.5 0.0 copy-start.1
  237.5 0.9 copy.47
  238.4 0.0 copy-done.6
  238.4 0.6 copy.48
  239.0 0.0 copy-done.5
  239.0 0.6 copy.49
  239.6 0.0 copy-done.4
  239.6 0.6 copy.50
  240.3 0.0 copy-done.3
  240.3 0.6 copy.51
  240.9 0.0 copy-done.2
  240.9 0.7 copy.52
  241.6 0.0 copy-done.1
  241.6 0.7 copy.53
  (4 shorter events, 0.0 us)
Async XLA Ops:
  234.7 2.7 %copy-start = (bf16[4,128,768]{2,1,0:T(8,128)(2,1)S(1)}, bf16[4,128,768]{2,1,0:T(8,128)(2,1)}, u32[]{:S(2)}) copy-start(bf16[4,128,768]{2,1,0:T(8,128)(2,1)} %get-tuple-element.109) | copy-start | bytes 2359300
  237.4 0.9 copy-start.6
  237.4 1.6 copy-start.5
  237.4 2.2 copy-start.4
  237.5 2.8 %copy-start.3 = (f32[24,768]{1,0:T(8,128)S(1)}, f32[24,768]{1,0:T(8,128)}, u32[]{:S(2)}) copy-start(f32[24,768]{1,0:T(8,128)} %get-tuple-element.115) | copy-start | bytes 221188
  237.5 3.4 %copy-start.2 = (f32[24,3072]{1,0:T(8,128)S(1)}, f32[24,3072]{1,0:T(8,128)}, u32[]{:S(2)}) copy-start(f32[24,3072]{1,0:T(8,128)} %get-tuple-element.119) | copy-start | bytes 884740
  237.5 4.2 %copy-start.1 = (f32[96,768]{1,0:T(8,128)S(1)}, f32[96,768]{1,0:T(8,128)}, u32[]{:S(2)}) copy-start(f32[96,768]{1,0:T(8,128)} %get-tuple-element.121) | copy-start | bytes 884740
where the time goes:
time: 243 us; the launch traced here: 242 us
  Pallas kernels  224 us (92%)
  local copies, waits for them, and re-layouts  16.5 us (7%)
    pallas_call x1, Pallas kernels, backward(): pl.pallas_call(backward_kernel, out_shape=[jax.ShapeDtypeStruct(shape, ki...  117 us
    pallas_call x1, Pallas kernels, forward(): pl.pallas_call(forward_kernel, out_shape=[jax.ShapeDtypeStruct(shape, kin...  107 us
    unnamed x22, local copies, waits for them, and re-layouts  7.59 us

commit v1 on v0

--- a/solution.py
+++ b/solution.py
@@ -260,8 +260,8 @@
             in_order((side, 1)),
             in_order((far, 0)),
             in_order((side, 2)),
+            in_order((side, 3), (core, 0)),
             in_order((far, 1)),
-            in_order((side, 3), (core, 0)),
             in_order((far, 2)),
             in_order((far, 3), (core, 1), (core, 2)),
             in_order((core, 3)),
@@ -285,6 +285,109 @@
     return [DMA((3,)), DMA((3,))] + [DMA((2, 4))] * 4 + [DMA((4,))] * 2
 
 
+def split_mid(ref, which):
+    width = ref.shape[-1]
+    cut = width // 384 * 128
+    return ref.at[..., pl.ds(which * cut, (cut, width - cut)[which])]
+
+
+class GatherMid:
+    def __init__(self, own, buf, sems, place):
+        self.own, self.buf, self.place = own, buf, place
+        self.zs, self.zr, self.ss, self.sr, self.hs, self.hr, self.fs, self.fr, self.cs, self.cr = sems
+
+    def z_copy(self, j):
+        z, x, y, c = self.place
+        there = (z ^ j, x, y, c)
+        return remote(self.own, self.buf.at[z, x, y, c], self.zs.at[j - 1], self.zr.at[j - 1], there)
+
+    def side_copy(self, axis):
+        z, x, y, c = self.place
+        there = (z, 1 - x, y, c) if axis == 0 else (z, x, 1 - y, c)
+        source = split_mid(self.own, axis)
+        return remote(source, split_mid(self.buf.at[z, x, y, c], axis), self.ss.at[axis], self.sr.at[axis], there)
+
+    def half_copy(self, j, axis):
+        z, x, y, c = self.place
+        part = self.buf.at[z, 1 - x, y, c] if axis == 0 else self.buf.at[z, x, 1 - y, c]
+        part = split_mid(part, axis)
+        return remote(part, part, self.hs.at[axis, j - 1], self.hr.at[axis, j - 1], (z ^ j, x, y, c))
+
+    def far_copy(self, j, axis):
+        z, x, y, c = self.place
+        if axis == 0:
+            part, there = self.buf.at[z ^ j, :, y, c], (z, x, 1 - y, c)
+        else:
+            part, there = self.buf.at[z ^ j, x, :, c], (z, 1 - x, y, c)
+        part = split_mid(part, axis)
+        return remote(part, part, self.fs.at[axis, j], self.fr.at[axis, j], there)
+
+    def core_copy(self, k):
+        z, x, y, c = self.place
+        part = self.buf.at[:, (x, 1 - x, x, 1 - x)[k], (y, y, 1 - y, 1 - y)[k], c]
+        return remote(part, part, self.cs.at[k], self.cr.at[k], (z, x, y, 1 - c))
+
+    def start(self):
+        for axis in (0, 1):
+            self.side_copy(axis).start()
+        for j in (1, 2, 3):
+            self.z_copy(j).start()
+
+    def turn(self):
+        for axis in (0, 1):
+            self.side_copy(axis).wait_recv()
+            for j in (1, 2, 3):
+                self.half_copy(j, axis).start()
+        for axis in (0, 1):
+            self.far_copy(0, axis).start()
+
+    def far(self, j):
+        self.z_copy(j).wait_recv()
+        for axis in (0, 1):
+            self.half_copy(j, axis).wait_recv()
+            self.far_copy(j, axis).start()
+
+    def core(self, k):
+        if k:
+            for j in range(4):
+                for axis in (0, 1):
+                    self.far_copy(j, axis).wait_recv()
+            for k in (1, 2, 3):
+                self.core_copy(k).start()
+        else:
+            self.core_copy(0).start()
+
+    def steps(self):
+        far, core = self.far, self.core
+        return [
+            in_order((self.turn,)),
+            in_order((far, 1)),
+            in_order((far, 2)),
+            in_order((far, 3), (core, 0)),
+            in_order((core, 1)),
+        ]
+
+    def arrive(self):
+        for k in range(4):
+            self.core_copy(k).wait_recv()
+
+    def finish(self):
+        for axis in (0, 1):
+            self.side_copy(axis).wait_send()
+        for j in (1, 2, 3):
+            self.z_copy(j).wait_send()
+            for axis in (0, 1):
+                self.half_copy(j, axis).wait_send()
+        for j in range(4):
+            for axis in (0, 1):
+                self.far_copy(j, axis).wait_send()
+            self.core_copy(j).wait_send()
+
+
+def mid_sems():
+    return [DMA((3,))] * 2 + [DMA((2,))] * 2 + [DMA((2, 3))] * 2 + [DMA((2, 4))] * 2 + [DMA((4,))] * 2
+
+
 def lanes(shape):
     return lax.broadcasted_iota(jnp.int32, shape, len(shape) - 1)
 
@@ -342,9 +445,9 @@
 
 
 def forward_kernel(
-    tokens, grads, live, slots, w_q, w_k, w_v, w_o, w_1, w_2, small_in,
+    tokens, grads, ids, mask, w_q, w_k, w_v, w_o, w_1, w_2, small_in,
     qkv_out, lse, x_out, att_out, normed1_out, low_out, act_out, slope_out, normed2_out,
-    factors, bias, q_out, k_out, v_out, o_out, w1_out, w2_out, grad_pages, layer_slots,
+    factors, bias, q_out, k_out, v_out, o_out, w1_out, w2_out, grad_pages, layer_slots, slots, live,
     small, a_buf, w1_buf, w2_buf, x_buf, qkv, att, normed1, low, act, slope, second, normed2, layer, bias1,
     local, ts, tr, gs, gr, outs, *sems,
 ):
@@ -376,9 +479,10 @@
     token_copies = [page_copy(tokens, x_buf, ts, tr, j) for j in range(3)]
     grad_copies = [page_copy(grads, grad_pages, gs, gr, j) for j in range(3)]
     gathers = [
-        Gather(own, buf, sems[8 * i : 8 * i + 8], place)
-        for i, (own, buf) in enumerate(
-            [(small_in, small), (a_buf.at[here], a_buf), (w_1, w1_buf), (w_2, w2_buf)]
+        kind(own, buf, sems[8 * i :][: 8 if kind is Gather else 10], place)
+        for i, (kind, own, buf) in enumerate(
+            [(Gather, small_in, small), (Gather, a_buf.at[here], a_buf)]
+            + [(Gather, w_1, w1_buf), (GatherMid, w_2, w2_buf)]
         )
     ]
     vectors, atts, inner, outer = gathers
@@ -388,17 +492,25 @@
     vectors.start()
     for copy in token_copies:
         copy.start()
-    later_1, later_2 = inner.steps(), outer.steps()
-    for i, (first, other) in enumerate(zip(vectors.steps(), atts.steps())):
-        other()
-        first()
-        if i == 2:
-            inner.start()
-        if i == 5:
-            outer.start()
-        if i == 6:
-            later_1[0]()
-    for copy in copies[5:]:
+    inner.start()
+    outer.start()
+    slot_cap = grads.shape[1]
+    hot = (rows_of((8, length)) == ids[pl.ds(me, 1), :]).astype(F32)
+    earlier = (rows_of((length, length)) < lanes((length, length))).astype(BF16)
+    rank = dot(hot.astype(BF16), earlier) + (rows_of((8, length)) * slot_cap).astype(F32)
+    slots[...] = jnp.sum(hot * rank, axis=0, keepdims=True).astype(jnp.int32)
+    live[...] = jnp.broadcast_to(mask[pl.ds(me, 1), :].astype(F32), (8, length)).T[:, 0:1]
+    steps_0, steps_1, steps_2 = atts.steps(), inner.steps(), outer.steps()
+    behind = {3: [steps_1[0]], 4: [steps_1[1]], 5: [steps_1[2], steps_2[0]], 6: [steps_1[3]]}
+    for i, (main, extra) in enumerate(zip(steps_0, vectors.steps())):
+        main()
+        extra()
+        if i == 3:
+            for copy in copies[5:7]:
+                copy.wait()
+        for step in behind.get(i, ()):
+            step()
+    for copy in copies[7:]:
         copy.wait()
     for copy in grad_copies:
         copy.start()
@@ -416,8 +528,7 @@
     for i, ref in enumerate((q_out, k_out, v_out, o_out)):
         out.send(a_buf.at[:, :, :, :, :, pl.ds(i * feat, feat)], ref)
     out.send(x_rows, x_out)
-    for step in later_1[1:3]:
-        step()
+    steps_1[4]()
 
     def project(j, _):
         start = pl.multiple_of(j * TILE, TILE)
@@ -430,16 +541,8 @@
 
     lax.fori_loop(0, 3 * feat // TILE, project, 0)
     out.send(qkv, qkv_out)
-    for step in later_1[3:5]:
-        step()
-    under = [
-        [later_1[5], later_2[0]],
-        [later_1[6], later_2[1], later_2[2]],
-        [later_1[7], later_2[3]],
-        [later_2[4]],
-        [later_2[5]],
-        [later_2[6]],
-    ]
+    steps_1[5]()
+    under = {0: steps_1[6], 2: steps_1[7], 3: steps_2[1], 6: steps_2[2], 9: steps_2[3]}
     scale = HEAD_DIM**-0.5
 
     def pair(p, _):
@@ -458,10 +561,11 @@
             probs = (shifted * (1.0 / total)).astype(BF16)
             mixed.append(dot_rows(v, probs))
             lse[pl.ds(2 * p + h, 1), :] = top + jnp.log(total)
+            for at, step in under.items():
+                if at % 2 == h:
+                    pl.when(p == at // 2)(step)
         both = jnp.where(rows_of(mixed[0].shape) < HEAD_DIM, mixed[0], mixed[1])
         att[:, pl.ds(start, 128)] = both.T.astype(BF16)
-        for i, steps in enumerate(under):
-            pl.when(p == i)(in_order(*[(step,) for step in steps]))
         return 0
 
     lax.fori_loop(0, pairs, pair, 0)
@@ -483,7 +587,6 @@
     out.send(low, low_out)
     inner.arrive()
     out.send(w1_buf, w1_out)
-    later_2[7]()
 
     def ffn_in(j, _):
         block = block_of(j, TILE)
@@ -495,6 +598,7 @@
     lax.fori_loop(0, inner_width // TILE, ffn_in, 0)
     out.send(act, act_out)
     out.send(slope, slope_out)
+    steps_2[4]()
     outer.arrive()
     out.send(w2_buf, w2_out)
 
@@ -534,8 +638,8 @@
     out.wait()
 
 
-def forward(tokens, grads, live, slots, w_q, w_k, w_v, w_o, w_1, w_2, small):
-    length, feat, inner_width = slots.shape[1], tokens.shape[-1], w_1.shape[1]
+def forward(tokens, grads, ids, mask, w_q, w_k, w_v, w_o, w_1, w_2, small):
+    length, feat, inner_width = ids.shape[1], tokens.shape[-1], w_1.shape[1]
     anywhere = pl.BlockSpec(memory_space=pl.ANY)
     vmem = pl.BlockSpec(memory_space=pltpu.VMEM)
     grid = (4, 2, 2, 2)
@@ -556,6 +660,7 @@
     results += [(grid + w_q.shape, BF16, anywhere)] * 4
     results += [(grid + w_1.shape, BF16, anywhere), (grid + w_2.shape, BF16, anywhere)]
     results += [(grads.shape, BF16, anywhere), (grads.shape, BF16, vmem)]
+    results += [((1, length), jnp.int32, vmem), ((length, 1), F32, vmem)]
     return pl.pallas_call(
         forward_kernel,
         out_shape=[jax.ShapeDtypeStruct(shape, kind) for shape, kind, _ in results],
@@ -584,12 +689,13 @@
             DMA((3,)),
             DMA((14,)),
         ]
-        + gather_sems() * 4,
+        + gather_sems() * 3
+        + mid_sems(),
         compiler_params=pltpu.CompilerParams(
             collective_id=0, has_side_effects=True, vmem_limit_bytes=VMEM_LIMIT
         ),
         name="forward",
-    )(tokens, grads, live, slots, w_q, w_k, w_v, w_o, w_1, w_2, small)
+    )(tokens, grads, ids, mask, w_q, w_k, w_v, w_o, w_1, w_2, small)
 
 
 def add_into(dst, src, lead):
@@ -609,121 +715,82 @@
 
 
 class Reduce:
-    def __init__(self, part, bufs, sems, place, write, by_z):
+    def __init__(self, part, bufs, sems, place, write):
         self.part, self.place, self.write = part, place, write
         self.got_core, self.got_1, self.got_2, self.got_z = bufs[0], bufs[1:3], bufs[3:5], bufs[5]
         self.cs, self.cr, self.fs, self.fr, self.ss, self.sr, self.zs, self.zr = sems
-        self.chunks = (3, 2, 1, 0) if by_z else (0,)
-        self.by_z = by_z
-
-    def at(self, j):
-        return self.place[0] ^ j if self.by_z else slice(None)
-
-    def lead(self, *rest):
-        return rest if self.by_z else (4,) + rest
-
-    def core_copy(self, j):
-        z, x, y, c = self.place
-        zi = self.at(j)
+
+    def core_copy(self):
+        z, x, y, c = self.place
         there = (z, x, y, 1 - c)
-        return remote(self.part.at[zi, :, :, 1 - c], self.got_core.at[zi], self.cs.at[j], self.cr.at[j], there)
-
-    def first_copy(self, j, axis):
-        z, x, y, c = self.place
-        zi = self.at(j)
+        return remote(self.part.at[:, :, :, 1 - c], self.got_core, self.cs.at[0], self.cr.at[0], there)
+
+    def first_copy(self, axis):
+        z, x, y, c = self.place
         if axis == 0:
-            part, there = self.part.at[zi, :, 1 - y, c], (z, x, 1 - y, c)
+            part, there = self.part.at[:, :, 1 - y, c], (z, x, 1 - y, c)
         else:
-            part, there = self.part.at[zi, 1 - x, :, c], (z, 1 - x, y, c)
-        return remote(split_ref(part, axis), self.got_1[axis].at[zi], self.fs.at[axis, j], self.fr.at[axis, j], there)
-
-    def second_copy(self, j, axis):
-        z, x, y, c = self.place
-        zi = self.at(j)
+            part, there = self.part.at[:, 1 - x, :, c], (z, 1 - x, y, c)
+        return remote(split_ref(part, axis), self.got_1[axis], self.fs.at[axis], self.fr.at[axis], there)
+
+    def second_copy(self, axis):
+        z, x, y, c = self.place
         if axis == 0:
-            part, there = self.part.at[zi, 1 - x, y, c], (z, 1 - x, y, c)
+            part, there = self.part.at[:, 1 - x, y, c], (z, 1 - x, y, c)
         else:
-            part, there = self.part.at[zi, x, 1 - y, c], (z, x, 1 - y, c)
-        return remote(split_ref(part, axis), self.got_2[axis].at[zi], self.ss.at[axis, j], self.sr.at[axis, j], there)
+            part, there = self.part.at[:, x, 1 - y, c], (z, x, 1 - y, c)
+        return remote(split_ref(part, axis), self.got_2[axis], self.ss.at[axis], self.sr.at[axis], there)
 
     def z_copy(self, j):
         z, x, y, c = self.place
         part = self.part.at[z ^ j, x, y, c]
         return remote(part, self.got_z.at[j - 1], self.zs.at[j - 1], self.zr.at[j - 1], (z ^ j, x, y, c))
 
-    def send(self, j):
-        self.core_copy(j).start()
-
     def send_all(self):
-        for j in self.chunks:
-            self.send(j)
-
-    def first(self, j):
-        z, x, y, c = self.place
-        zi = self.at(j)
-        self.core_copy(j).wait_recv()
-        add_into(self.part.at[zi, :, :, c], self.got_core.at[zi], self.lead(2, 2))
-        for axis in (0, 1):
-            self.first_copy(j, axis).start()
-
-    def second(self, j):
-        z, x, y, c = self.place
-        zi = self.at(j)
-        for axis in (0, 1):
-            self.first_copy(j, axis).wait_recv()
-            part = self.part.at[zi, :, y, c] if axis == 0 else self.part.at[zi, x, :, c]
-            add_into(split_ref(part, axis), self.got_1[axis].at[zi], self.lead(2))
-            self.second_copy(j, axis).start()
-
-    def along_z(self, j):
-        z, x, y, c = self.place
-        zi = self.at(j)
-        for axis in (0, 1):
-            self.second_copy(j, axis).wait_recv()
-            part = split_ref(self.part.at[zi, x, y, c], axis)
-            got = self.got_2[axis].at[zi]
-            if self.by_z:
-                part[...] = (part[...].astype(F32) + got[...].astype(F32)).astype(BF16)
-            else:
-                add_into(part, got, (4,))
-        for i in (1, 2, 3):
-            if not self.by_z or i == j:
-                self.z_copy(i).start()
+        self.core_copy().start()
+
+    def first(self):
+        z, x, y, c = self.place
+        self.core_copy().wait_recv()
+        add_into(self.part.at[:, :, :, c], self.got_core, (4, 2, 2))
+        for axis in (0, 1):
+            self.first_copy(axis).start()
+
+    def second(self):
+        z, x, y, c = self.place
+        for axis in (0, 1):
+            self.first_copy(axis).wait_recv()
+            part = self.part.at[:, :, y, c] if axis == 0 else self.part.at[:, x, :, c]
+            add_into(split_ref(part, axis), self.got_1[axis], (4, 2))
+            self.second_copy(axis).start()
+
+    def along_z(self):
+        z, x, y, c = self.place
+        for axis in (0, 1):
+            self.second_copy(axis).wait_recv()
+            add_into(split_ref(self.part.at[:, x, y, c], axis), self.got_2[axis], (4,))
+        for j in (1, 2, 3):
+            self.z_copy(j).start()
 
     def last(self):
         z, x, y, c = self.place
         total = self.part[z, x, y, c].astype(F32)
-        for i in (1, 2, 3):
-            self.z_copy(i).wait_recv()
-            total = total + self.got_z[i - 1].astype(F32)
+        for j in (1, 2, 3):
+            self.z_copy(j).wait_recv()
+            total = total + self.got_z[j - 1].astype(F32)
         self.write(total)
 
-    def steps(self):
-        first, second, along = self.first, self.second, self.along_z
-        if not self.by_z:
-            return [in_order((first, 0)), in_order((second, 0)), in_order((along, 0)), in_order((self.last,))]
-        return [
-            in_order((first, 3)),
-            in_order((first, 2), (second, 3)),
-            in_order((first, 1), (second, 2), (along, 3)),
-            in_order((first, 0), (second, 1), (along, 2)),
-            in_order((second, 0), (along, 1)),
-            in_order((along, 0)),
-            in_order((self.last,)),
-        ]
-
     def finish(self):
-        for j in self.chunks:
-            self.core_copy(j).wait_send()
-            for axis in (0, 1):
-                self.first_copy(j, axis).wait_send()
-                self.second_copy(j, axis).wait_send()
-        for i in (1, 2, 3):
-            self.z_copy(i).wait_send()
+        self.core_copy().wait_send()
+        for axis in (0, 1):
+            self.first_copy(axis).wait_send()
+            self.second_copy(axis).wait_send()
+        for j in (1, 2, 3):
+            self.z_copy(j).wait_send()
 
 
 def reduce_sems():
-    return [DMA((4,))] * 2 + [DMA((2, 4))] * 4 + [DMA((3,))] * 2
+    return [DMA((1,))] * 2 + [DMA((2,))] * 4 + [DMA((3,))] * 2
 
 
 def reduce_bufs(rows, width):
@@ -735,6 +802,114 @@
         pltpu.VMEM(split_shape((4,) + shape, 0), BF16),
         pltpu.VMEM(split_shape((4,) + shape, 1), BF16),
         pltpu.VMEM((3,) + shape, BF16),
+    ]
+
+
+class ReduceMid:
+    def __init__(self, part, bufs, sems, place, write):
+        self.part, self.place, self.write = part, place, write
+        self.got_core, self.got_1, self.got_z, self.got_last = bufs[0], bufs[1:3], bufs[3:5], bufs[5]
+        self.cs, self.cr, self.fs, self.fr, self.zs, self.zr, self.ls, self.lr = sems
+
+    def core_copy(self, j):
+        z, x, y, c = self.place
+        zi = z ^ j
+        there = (z, x, y, 1 - c)
+        return remote(self.part.at[zi, :, :, 1 - c], self.got_core.at[zi], self.cs.at[j], self.cr.at[j], there)
+
+    def mine(self, zi, axis, other=0):
+        z, x, y, c = self.place
+        part = self.part.at[zi, :, abs(other - y), c] if axis == 0 else self.part.at[zi, abs(other - x), :, c]
+        return split_mid(part, axis)
+
+    def first_copy(self, j, axis):
+        z, x, y, c = self.place
+        zi = z ^ j
+        there = (z, x, 1 - y, c) if axis == 0 else (z, 1 - x, y, c)
+        return remote(self.mine(zi, axis, 1), self.got_1[axis].at[zi], self.fs.at[axis, j], self.fr.at[axis, j], there)
+
+    def z_copy(self, j, axis):
+        z, x, y, c = self.place
+        return remote(
+            self.mine(z ^ j, axis), self.got_z[axis].at[j - 1], self.zs.at[axis, j - 1], self.zr.at[axis, j - 1], (z ^ j, x, y, c)
+        )
+
+    def last_copy(self, axis):
+        z, x, y, c = self.place
+        if axis == 0:
+            part, there = self.part.at[z, 1 - x, y, c], (z, 1 - x, y, c)
+        else:
+            part, there = self.part.at[z, x, 1 - y, c], (z, x, 1 - y, c)
+        return remote(split_mid(part, axis), split_mid(self.got_last, axis), self.ls.at[axis], self.lr.at[axis], there)
+
+    def send(self, j):
+        self.core_copy(j).start()
+
+    def send_all(self):
+        for j in (3, 2, 1, 0):
+            self.send(j)
+
+    def first(self, j):
+        z, x, y, c = self.place
+        zi = z ^ j
+        self.core_copy(j).wait_recv()
+        add_into(self.part.at[zi, :, :, c], self.got_core.at[zi], (2, 2))
+        for axis in (0, 1):
+            self.first_copy(j, axis).start()
+
+    def turn(self, j):
+        zi = self.place[0] ^ j
+        for axis in (0, 1):
+            self.first_copy(j, axis).wait_recv()
+            add_into(self.mine(zi, axis), self.got_1[axis].at[zi], (2,))
+            if j:
+                self.z_copy(j, axis).start()
+
+    def fold(self):
+        z, x, y, c = self.place
+        for axis in (0, 1):
+            for j in (1, 2, 3):
+                self.z_copy(j, axis).wait_recv()
+            mine, got = self.mine(z, axis), self.got_z[axis]
+
+            def add(i, _, mine=mine, got=got):
+                total = mine[i].astype(F32) + got[0, i].astype(F32)
+                mine[i] = (total + got[1, i].astype(F32) + got[2, i].astype(F32)).astype(BF16)
+                return 0
+
+            lax.fori_loop(0, 2, add, 0)
+            self.last_copy(axis).start()
+
+    def last(self):
+        z, x, y, c = self.place
+        for axis in (0, 1):
+            self.last_copy(axis).wait_recv()
+        self.write(self.part[z, x, y, c].astype(F32) + self.got_last[...].astype(F32))
+
+    def finish(self):
+        for j in range(4):
+            self.core_copy(j).wait_send()
+            for axis in (0, 1):
+                self.first_copy(j, axis).wait_send()
+                if j:
+                    self.z_copy(j, axis).wait_send()
+        for axis in (0, 1):
+            self.last_copy(axis).wait_send()
+
+
+def reduce_mid_sems():
+    return [DMA((4,))] * 2 + [DMA((2, 4))] * 2 + [DMA((2, 3))] * 2 + [DMA((2,))] * 2
+
+
+def reduce_mid_bufs(rows, width):
+    cut = width // 384 * 128
+    return [
+        pltpu.VMEM((4, 2, 2, rows, width), BF16),
+        pltpu.VMEM((4, 2, rows, cut), BF16),
+        pltpu.VMEM((4, 2, rows, width - cut), BF16),
+        pltpu.VMEM((3, 2, rows, cut), BF16),
+        pltpu.VMEM((3, 2, rows, width - cut), BF16),
+        pltpu.VMEM((rows, width), BF16),
     ]
 
 
@@ -790,14 +965,13 @@
 
         return write
 
-    parts = [(g_2, whole(w2_out), True), (g_1, whole(w1_out), True), (g_o, whole(o_out), False)]
-    parts += [(g_qkv.at[i], thirds(i), False) for i in range(GROUPS)]
-    parts += [(g_small, whole(small_out), False)]
+    parts = [(ReduceMid, g_2, whole(w2_out)), (ReduceMid, g_1, whole(w1_out)), (Reduce, g_o, whole(o_out))]
+    parts += [(Reduce, g_qkv.at[i], thirds(i)) for i in range(GROUPS)]
+    parts += [(Reduce, g_small, whole(small_out))]
     sums_2, sum_1, sum_o, *sum_qkv, sum_small = reduces = [
-        Reduce(part, bufs[6 * i : 6 * i + 6], sems[8 * i : 8 * i + 8], place, write, by_z)
-        for i, (part, write, by_z) in enumerate(parts)
+        kind(part, bufs[6 * i : 6 * i + 6], sems[8 * i : 8 * i + 8], place, write)
+        for i, (kind, part, write) in enumerate(parts)
     ]
-    steps_2, steps_1, steps_o, *steps_qkv, steps_small = [one.steps() for one in reduces]
 
     sums[...] = jnp.zeros_like(sums)
     sums1[...] = jnp.zeros_like(sums1)
@@ -835,13 +1009,16 @@
         part = dot_rows(act[:, block_of(zi, width)], second[...])
         g_2[zi] = part.astype(BF16).reshape(g_2.shape[1:])
         sums_2.send(j)
+        for k in (1, 2, 3):
+            pl.when(i == k)(in_order((sums_2.first, 4 - k)))
         return 0
 
     lax.fori_loop(0, 4, outer_grad, 0)
+    sums_2.first(0)
     for copy in loads[6:9]:
         copy.wait()
     turned[...] = low[...].T
-    when_2 = {2: 0, 4: 1, 6: 2, 8: 3, 10: 4}
+    under_inner = {5: [(sums_2.turn, 3)], 10: [(sums_2.turn, 2)]}
 
     def inner_grad(i, _):
         block = block_of(i, TILE)
@@ -851,8 +1028,8 @@
         sums1[0:1, block] = jnp.sum(inner_low.astype(F32), axis=0, keepdims=True)
         part = dot(turned[...], inner_low)
         g_1[:, :, :, :, :, block] = part.astype(BF16).reshape(g_1.shape[:-1] + (TILE,))
-        for at, index in when_2.items():
-            pl.when(i == at)(steps_2[index])
+        for at, calls in under_inner.items():
+            pl.when(i == at)(in_order(*calls))
         return 0
 
     lax.fori_loop(0, inner_width // TILE, inner_grad, 0)
@@ -865,7 +1042,6 @@
         copy.start()
     for copy in loads[9:]:
         copy.wait()
-    steps_2[5]()
 
     def hidden_grad(i, _):
         half_width = feat // 2
@@ -875,7 +1051,7 @@
         return 0
 
     lax.fori_loop(0, 2, hidden_grad, 0)
-    steps_1[0]()
+    in_order((sum_1.first, 3), (sum_1.first, 2), (sums_2.turn, 1))()
     first = second
 
     def norm_one(i, _):
@@ -891,6 +1067,7 @@
         return 0
 
     lax.fori_loop(0, length // rows, norm_one, 0)
+    in_order((sum_1.first, 1), (sum_1.first, 0))()
     for copy in slabs:
         copy.wait()
     g_o[...] = dot_rows(att[...], first[...]).astype(BF16).reshape(g_o.shape)
@@ -904,7 +1081,7 @@
 
     lax.fori_loop(0, length // rows, att_grad, 0)
     turned[...] = x[...].T
-    steps_1[1]()
+    in_order((sums_2.turn, 0), (sum_o.first,))()
     scale = HEAD_DIM**-0.5
 
     def pair(p):
@@ -923,6 +1100,9 @@
             up = dot_cols(jnp.where(keep, v, zero), g)
             inner_sum = jnp.sum(probs * up, axis=0, keepdims=True)
             grad_scores = (probs * (up - inner_sum)).astype(BF16)
+            for at, calls in under.items():
+                if at % 2 == h:
+                    pl.when(p == at // 2)(in_order(*calls))
             results.append((dot_rows(k, grad_scores), dot(grad_scores, q), dot(probs.astype(BF16), g)))
         (q_0, k_0, v_0), (q_1, k_1, v_1) = results
         d_q = jnp.where(rows_of(q_0.shape) < HEAD_DIM, q_0, q_1) * scale
@@ -930,21 +1110,19 @@
         d_qkv[:, pl.ds(feat + start, 128)] = jnp.where(low_lane, k_0, k_1).astype(BF16)
         d_qkv[:, pl.ds(2 * feat + start, 128)] = jnp.where(low_lane, v_0, v_1).astype(BF16)
 
-    under = [
-        [steps_1[2], steps_2[6]],
-        [steps_1[3], steps_o[0]],
-        [steps_1[4], steps_o[1]],
-        [steps_1[5], steps_qkv[0][0]],
-        [steps_o[2], steps_qkv[0][1]],
-        [steps_1[6], steps_qkv[1][0]],
-    ]
+    under = {
+        2: [(sum_1.turn, 3)],
+        4: [(sum_1.turn, 2)],
+        5: [(sum_qkv[0].first,)],
+        7: [(sum_1.turn, 1)],
+        9: [(sums_2.fold,), (sum_qkv[1].first,)],
+        10: [(sum_1.turn, 0)],
+        11: [(sums_2.last,)],
+    }
 
     def group(i, _):
         def one(j, _):
-            p = 2 * i + j
-            pair(p)
-            for at, steps in enumerate(under):
-                pl.when(p == at)(in_order(*[(step,) for step in steps]))
+            pair(2 * i + j)
             return 0
 
         lax.fori_loop(0, 2, one, 0)
@@ -966,7 +1144,7 @@
         part = sums1[:, i * (inner_width // 4) : (i + 1) * (inner_width // 4)]
         g_small[i, :, :, :, 8:16, :] = pack_rows(part, inner_width // 32, 8).reshape(2, 2, 2, 8, 128)
     sum_small.send_all()
-    steps_qkv[2][0]()
+    sum_qkv[2].first()
 
     def token_grad(i, _):
         block = block_of(i, rows)
@@ -985,19 +1163,27 @@
         copy.start()
     token_own = pltpu.make_async_copy(grad_tokens.at[me], tokens_out.at[me], local.at[19])
     token_own.start()
-    steps_small[0]()
-    steps_qkv[1][1]()
-    steps_o[3]()
-    steps_qkv[0][2]()
-    steps_qkv[2][1]()
-    steps_small[1]()
-    steps_qkv[1][2]()
-    steps_qkv[0][3]()
-    steps_qkv[2][2]()
-    steps_small[2]()
-    steps_qkv[1][3]()
-    steps_qkv[2][3]()
-    steps_small[3]()
+    thirds_0, thirds_1, thirds_2 = sum_qkv
+    in_order(
+        (sum_small.first,),
+        (sum_o.second,),
+        (thirds_0.second,),
+        (sum_o.along_z,),
+        (thirds_1.second,),
+        (thirds_0.along_z,),
+        (sum_small.second,),
+        (sum_1.fold,),
+        (thirds_2.second,),
+        (thirds_1.along_z,),
+        (sum_small.along_z,),
+        (sum_o.last,),
+        (thirds_2.along_z,),
+        (sum_1.last,),
+        (thirds_0.last,),
+        (thirds_1.last,),
+        (sum_small.last,),
+        (thirds_2.last,),
+    )()
     for copy in layer_copies + token_copies:
         copy.wait()
     layer_own.wait()
@@ -1039,9 +1225,9 @@
         ((8, inner_width), F32),
     ]
     bufs, sems = [], []
-    for size in sizes:
-        bufs += reduce_bufs(*size)
-        sems += reduce_sems()
+    for i, size in enumerate(sizes):
+        bufs += reduce_mid_bufs(*size) if i < 2 else reduce_bufs(*size)
+        sems += reduce_mid_sems() if i < 2 else reduce_sems()
     outs = [(grad_pages.shape, BF16, anywhere), (tokens_shape, BF16, anywhere)]
     outs += [(small, F32, vmem)] * 4 + [(inner, F32, vmem), (outer, F32, vmem), ((16, 128), F32, vmem)]
     return pl.pallas_call(
@@ -1061,31 +1247,59 @@
 
 
 def small_shard(weights):
-    rows = [jnp.pad(weights[i], (0, 128 - weights[i].shape[0])) for i in SMALL_ORDER]
-    rows += [jnp.zeros_like(rows[0])] * (16 - len(rows))
-    return jnp.stack(rows)
+    rows = []
+    for i in SMALL_ORDER:
+        rows += [weights[i], jnp.zeros((128 - weights[i].shape[0],), BF16)]
+    rows.append(jnp.zeros((128 * (16 - len(SMALL_ORDER)),), BF16))
+    return jnp.concatenate(rows).reshape(16, 128)
 
 
 SMALL_ORDER = (1, 4, 6, 7, 8, 12, 13, 14, 10)
 
 
+def finish_kernel(count, *refs):
+    ins, outs, stages, sems = refs[:count], refs[count : 2 * count], refs[2 * count : 3 * count], refs[3 * count]
+    inward = [pltpu.make_async_copy(i, s, sems.at[0, n]) for n, (i, s) in enumerate(zip(ins, stages))]
+    outward = [pltpu.make_async_copy(s, o, sems.at[1, n]) for n, (s, o) in enumerate(zip(stages, outs))]
+    for copy in inward:
+        copy.start()
+    for first, second in zip(inward, outward):
+        first.wait()
+        second.start()
+    for copy in outward:
+        copy.wait()
+
+
+def finish(arrays):
+    count = len(arrays)
+    anywhere = pl.BlockSpec(memory_space=pl.ANY)
+
+    def body(*refs):
+        finish_kernel(count, *refs)
+
+    return pl.pallas_call(
+        body,
+        out_shape=[jax.ShapeDtypeStruct(a.shape, a.dtype) for a in arrays],
+        in_specs=[anywhere] * count,
+        out_specs=[anywhere] * count,
+        scratch_shapes=[pltpu.VMEM(a.shape, a.dtype) for a in arrays] + [DMA((2, count))],
+        compiler_params=pltpu.CompilerParams(vmem_limit_bytes=VMEM_LIMIT),
+        name="finish",
+    )(*arrays)
+
+
 def by_kernels(tokens, band_ids, page_mask, weights, grad_output):
-    bands = lax.axis_size("band")
-    me = lax.axis_index("band")
-    slot_cap, feat = grad_output.shape[1:]
-    ids = lax.dynamic_slice_in_dim(band_ids, me, 1, 0)
-    live = lax.dynamic_slice_in_dim(page_mask, me, 1, 0)
-    slots = page_slots(ids, bands, slot_cap)
     large = [weights[i] for i in (0, 2, 3, 5, 9, 11)]
-    got = forward(tokens, grad_output, live.reshape(-1, 1), slots, *large, small_shard(weights))
-    saved, full, grad_slots, layer_slots = got[:11], got[11:17], got[17], got[18]
+    got = forward(tokens, grad_output, band_ids, page_mask, *large, small_shard(weights))
+    saved, full, (grad_slots, layer_slots, slots, live) = got[:11], got[11:17], got[17:]
     full = [w if i == 4 else w.reshape(-1, w.shape[-1]) for i, w in enumerate(full)]
-    sums = backward(saved, full, grad_slots, layer_slots, slots, live.reshape(-1, 1), tokens.shape)
+    sums = backward(saved, full, grad_slots, layer_slots, slots, live, tokens.shape)
     grads = [None] * len(weights)
-    for i, total in zip((0, 2, 3, 5, 9, 11), sums[2:8]):
-        grads[i] = total
     for row, i in enumerate(SMALL_ORDER):
         grads[i] = sums[8][row, : weights[i].shape[0]]
+    sums = finish(sums[:8])
+    for i, total in zip((0, 2, 3, 5, 9, 11), sums[2:]):
+        grads[i] = total
     return tuple(sums[:2]) + tuple(grads)
 
 

time: 243 us -> 217 us (0.89)
  Pallas kernels: 224 us -> 209 us
  local copies, waits for them, and re-layouts: 16.5 us -> 7.76 us
    pallas_call x1, Pallas kernels: 107 us -> 92.7 us  [forward(): pl.pallas_call(forward_kernel, out_shape=[jax.ShapeDtypeStruct(shape, kin...]
    unnamed x22 -> x2, local copies, waits for them, and re-layouts: 7.59 us -> 0.01 us
    concatenate x0 -> x1, local copies, waits for them, and re-layouts: none -> 6.69 us  [small_shard(): return jnp.concatenate(rows).reshape(16, 128)]
    another operation x9 -> x1, local copies, waits for them, and re-layouts: 4.58 us -> 0.01 us  [small_shard(): return jnp.stack(rows)]
    pallas_call x1, Pallas kernels: 117 us -> 113 us  [backward(): pl.pallas_call(backward_kernel, out_shape=[jax.ShapeDtypeStruct(shape, ki...]
    pallas_call x0 -> x1, Pallas kernels: none -> 3.24 us  [finish(): pl.pallas_call(body, out_shape=[jax.ShapeDtypeStruct(a.shape, a.dtype) fo...]
where the time goes in v1:
time: 217 us
  Pallas kernels  209 us (96%)
  local copies, waits for them, and re-layouts  7.76 us (4%)
    pallas_call x1, Pallas kernels, backward(): pl.pallas_call(backward_kernel, out_shape=[jax.ShapeDtypeStruct(shape, ki...  113 us
    pallas_call x1, Pallas kernels, forward(): pl.pallas_call(forward_kernel, out_shape=[jax.ShapeDtypeStruct(shape, kin...  92.7 us
    concatenate x1, local copies, waits for them, and re-layouts, small_shard(): return jnp.concatenate(rows).reshape(16, 128)  6.69 us

profile of v1, /device:TPU:0, one launch (start us, length us, event | category | flops | bytes accessed | tf_op | source)
XLA Modules:
  0.0 217.0 jit_solution(4494296868456346602)
XLA Ops:
  0.7 6.7 %concatenate.3 = bf16[2048]{0:T(1024)(128)(2,1)} concatenate(bf16[24]{0:T(256)(128)(2,1)} %param.24, bf16[104]{0:T(256)(128)(2,1)S(1)} %broadcast.3, bf16[24]{0:T(256)(128)(2,1)} %param.27, bf16[104]{0:T(256)(128)(2,1)S(1)} %broadcast.3, bf16[24]{0:T(256)(128)(2,1)} %param.29, bf16[104]{0:T(256)(128)(2,1)S(1)} %broadcast.3, bf16[24]{0:T(256)(128)(2,1)} %param.30, ...), dimensions={0} | concatenate | bytes 8192 | tf_op jit(solution)/shard_map/concatenate | solution.py:1254
  7.4 92.7 %forward.1 = (bf16[512,2304]{1,0:T(8,128)(2,1)}, f32[16,512]{1,0:T(8,128)}, bf16[512,768]{1,0:T(8,128)(2,1)}, bf16[512,768]{1,0:T(8,128)(2,1)}, f32[512,768]{1,0...) custom-call(bf16[4,128,768]{2,1,0:T(8,128)(2,1)} %tokens.1, ...), custom_call_target="tpu_custom_call" | custom-call | tf_op jit(solution)/shard_map/forward/pallas_call | solution.py:664
  100.1 112.5 %backward.1 = (bf16[4,256,768]{2,1,0:T(8,128)(2,1)}, bf16[4,128,768]{2,1,0:T(8,128)(2,1)}, f32[24,768]{1,0:T(8,128)}, f32[24,768]{1,0:T(8,128)}, f32[24,768]{1,0...) custom-call(bf16[512,2304]{1,0:T(8,128)(2,1)} %get-tuple-element.55.qkv_in, ...), custom_call_target="tpu_custom_call" | custom-call | tf_op jit(solution)/shard_map/backward/pallas_call | solution.py:1233
  212.7 0.0 copy-start
  212.7 3.2 %finish.1 = (bf16[4,256,768]{2,1,0:T(8,128)(2,1)}, bf16[4,128,768]{2,1,0:T(8,128)(2,1)}, f32[24,768]{1,0:T(8,128)}, f32[24,768]{1,0:T(8,128)}, f32[24,768]{1,0:T...) custom-call(bf16[4,256,768]{2,1,0:T(8,128)(2,1)} %get-tuple-element.76.refs_0_, ...), custom_call_target="tpu_custom_call" | custom-call | tf_op jit(solution)/shard_map/finish/pallas_call | solution.py:1280
  215.9 0.0 copy-done
  215.9 0.5 slice_bitcast_fusion.3
  216.4 0.5 slice_bitcast_fusion
  (3 shorter events, 0.0 us)
Async XLA Ops:
  212.7 3.3 %copy-start = (f32[16,128]{1,0:T(8,128)S(1)}, f32[16,128]{1,0:T(8,128)}, u32[]{:S(2)}) copy-start(f32[16,128]{1,0:T(8,128)} %get-tuple-element.87) | copy-start | bytes 24580

commit v2 on v1

--- a/solution.py
+++ b/solution.py
@@ -444,13 +444,13 @@
 TILE = 256
 
 
-def forward_kernel(
-    tokens, grads, ids, mask, w_q, w_k, w_v, w_o, w_1, w_2, small_in,
-    qkv_out, lse, x_out, att_out, normed1_out, low_out, act_out, slope_out, normed2_out,
-    factors, bias, q_out, k_out, v_out, o_out, w1_out, w2_out, grad_pages, layer_slots, slots, live,
-    small, a_buf, w1_buf, w2_buf, x_buf, qkv, att, normed1, low, act, slope, second, normed2, layer, bias1,
-    local, ts, tr, gs, gr, outs, *sems,
-):
+def forward_kernel(*refs):
+    vector_refs, refs = refs[: BIAS_ROWS + 1], refs[BIAS_ROWS + 1 :]
+    tokens, grads, ids, mask, w_q, w_k, w_v, w_o, w_1, w_2 = refs[:10]
+    qkv_out, lse, x_out, att_out, normed1_out, low_out, act_out, slope_out, normed2_out = refs[10:19]
+    factors, bias, q_out, k_out, v_out, o_out, w1_out, w2_out, grad_pages, layer_slots, slots, live = refs[19:31]
+    small, small_own, a_buf, w1_buf, w2_buf, x_buf, qkv, att, normed1, low, act, slope = refs[31:43]
+    second, normed2, layer, bias1, local, ts, tr, gs, gr, outs, *sems = refs[43:]
     place = z, x, y, c = my_place()
     me = y * 2 + c
     length, feat = low.shape
@@ -461,12 +461,17 @@
         pltpu.make_async_copy(src, dst, local.at[i])
         for i, (src, dst) in enumerate(
             [(w, a_buf.at[here + (slice(None), pl.ds(i * feat, feat))]) for i, w in enumerate((w_q, w_k, w_v, w_o))]
-            + [(small_in, small.at[here]), (w_1, w1_buf.at[here]), (w_2, w2_buf.at[here])]
+            + [(w_1, w1_buf.at[here]), (w_2, w2_buf.at[here])]
             + [(tokens.at[me], x_buf.at[me]), (grads.at[me], grad_pages.at[me])]
         )
     ]
     for copy in copies:
         copy.start()
+    small_own[...] = jnp.zeros_like(small_own)
+    for row, ref in enumerate(vector_refs):
+        size = ref.shape[0]
+        small_own[row : row + 1, 0:size] = ref[...].astype(F32).reshape(1, size)
+    small[here] = small_own[...].astype(BF16)
     meet(
         [(z ^ j, x, y, c) for j in (1, 2, 3)]
         + [(z, 1 - x, y, c), (z, x, 1 - y, c), (z, x, y, 1 - c), (z, x, 1 - y, 1 - c)]
@@ -481,12 +486,12 @@
     gathers = [
         kind(own, buf, sems[8 * i :][: 8 if kind is Gather else 10], place)
         for i, (kind, own, buf) in enumerate(
-            [(Gather, small_in, small), (Gather, a_buf.at[here], a_buf)]
+            [(Gather, small.at[here], small), (Gather, a_buf.at[here], a_buf)]
             + [(Gather, w_1, w1_buf), (GatherMid, w_2, w2_buf)]
         )
     ]
     vectors, atts, inner, outer = gathers
-    for copy in copies[:5]:
+    for copy in copies[:4]:
         copy.wait()
     atts.start()
     vectors.start()
@@ -506,11 +511,11 @@
         main()
         extra()
         if i == 3:
-            for copy in copies[5:7]:
+            for copy in copies[4:6]:
                 copy.wait()
         for step in behind.get(i, ()):
             step()
-    for copy in copies[7:]:
+    for copy in copies[6:]:
         copy.wait()
     for copy in grad_copies:
         copy.start()
@@ -638,7 +643,7 @@
     out.wait()
 
 
-def forward(tokens, grads, ids, mask, w_q, w_k, w_v, w_o, w_1, w_2, small):
+def forward(vectors, tokens, grads, ids, mask, w_q, w_k, w_v, w_o, w_1, w_2):
     length, feat, inner_width = ids.shape[1], tokens.shape[-1], w_1.shape[1]
     anywhere = pl.BlockSpec(memory_space=pl.ANY)
     vmem = pl.BlockSpec(memory_space=pltpu.VMEM)
@@ -657,6 +662,7 @@
         ((length, 256), F32, vmem),
         ((BIAS_ROWS, feat), F32, vmem),
     ]
+    small = (16, 128)
     results += [(grid + w_q.shape, BF16, anywhere)] * 4
     results += [(grid + w_1.shape, BF16, anywhere), (grid + w_2.shape, BF16, anywhere)]
     results += [(grads.shape, BF16, anywhere), (grads.shape, BF16, vmem)]
@@ -664,10 +670,11 @@
     return pl.pallas_call(
         forward_kernel,
         out_shape=[jax.ShapeDtypeStruct(shape, kind) for shape, kind, _ in results],
-        in_specs=[anywhere, anywhere, vmem, vmem] + [anywhere] * 7,
+        in_specs=[vmem] * len(vectors) + [anywhere, anywhere, vmem, vmem] + [anywhere] * 6,
         out_specs=[spec for _, _, spec in results],
         scratch_shapes=[
-            pltpu.VMEM(grid + small.shape, BF16),
+            pltpu.VMEM(grid + small, BF16),
+            pltpu.VMEM(small, F32),
             pltpu.VMEM(grid + (w_q.shape[0], 4 * feat), BF16),
             pltpu.VMEM(grid + w_1.shape, BF16),
             pltpu.VMEM(grid + w_2.shape, BF16),
@@ -682,7 +689,7 @@
             pltpu.VMEM((length, feat), F32),
             pltpu.VMEM((length, feat), BF16),
             pltpu.VMEM((8, inner_width), F32),
-            DMA((9,)),
+            DMA((8,)),
             DMA((3,)),
             DMA((3,)),
             DMA((3,)),
@@ -695,7 +702,7 @@
             collective_id=0, has_side_effects=True, vmem_limit_bytes=VMEM_LIMIT
         ),
         name="forward",
-    )(tokens, grads, ids, mask, w_q, w_k, w_v, w_o, w_1, w_2, small)
+    )(*vectors, tokens, grads, ids, mask, w_q, w_k, w_v, w_o, w_1, w_2)
 
 
 def add_into(dst, src, lead):
@@ -717,29 +724,19 @@
 class Reduce:
     def __init__(self, part, bufs, sems, place, write):
         self.part, self.place, self.write = part, place, write
-        self.got_core, self.got_1, self.got_2, self.got_z = bufs[0], bufs[1:3], bufs[3:5], bufs[5]
-        self.cs, self.cr, self.fs, self.fr, self.ss, self.sr, self.zs, self.zr = sems
+        self.got_core, self.got_plane, self.got_z = bufs
+        self.cs, self.cr, self.ps, self.pr, self.zs, self.zr = sems
 
     def core_copy(self):
         z, x, y, c = self.place
         there = (z, x, y, 1 - c)
         return remote(self.part.at[:, :, :, 1 - c], self.got_core, self.cs.at[0], self.cr.at[0], there)
 
-    def first_copy(self, axis):
-        z, x, y, c = self.place
-        if axis == 0:
-            part, there = self.part.at[:, :, 1 - y, c], (z, x, 1 - y, c)
-        else:
-            part, there = self.part.at[:, 1 - x, :, c], (z, 1 - x, y, c)
-        return remote(split_ref(part, axis), self.got_1[axis], self.fs.at[axis], self.fr.at[axis], there)
-
-    def second_copy(self, axis):
-        z, x, y, c = self.place
-        if axis == 0:
-            part, there = self.part.at[:, 1 - x, y, c], (z, 1 - x, y, c)
-        else:
-            part, there = self.part.at[:, x, 1 - y, c], (z, x, 1 - y, c)
-        return remote(split_ref(part, axis), self.got_2[axis], self.ss.at[axis], self.sr.at[axis], there)
+    def plane_copy(self, j):
+        z, x, y, c = self.place
+        px, py = x ^ (j // 2), y ^ (j % 2)
+        there = (z, px, py, c)
+        return remote(self.part.at[:, px, py, c], self.got_plane.at[j - 1], self.ps.at[j - 1], self.pr.at[j - 1], there)
 
     def z_copy(self, j):
         z, x, y, c = self.place
@@ -753,23 +750,22 @@
         z, x, y, c = self.place
         self.core_copy().wait_recv()
         add_into(self.part.at[:, :, :, c], self.got_core, (4, 2, 2))
-        for axis in (0, 1):
-            self.first_copy(axis).start()
-
-    def second(self):
-        z, x, y, c = self.place
-        for axis in (0, 1):
-            self.first_copy(axis).wait_recv()
-            part = self.part.at[:, :, y, c] if axis == 0 else self.part.at[:, x, :, c]
-            add_into(split_ref(part, axis), self.got_1[axis], (4, 2))
-            self.second_copy(axis).start()
+        for j in (3, 2, 1):
+            self.plane_copy(j).start()
 
     def along_z(self):
         z, x, y, c = self.place
-        for axis in (0, 1):
-            self.second_copy(axis).wait_recv()
-            add_into(split_ref(self.part.at[:, x, y, c], axis), self.got_2[axis], (4,))
         for j in (1, 2, 3):
+            self.plane_copy(j).wait_recv()
+        mine, got = self.part.at[:, x, y, c], self.got_plane
+
+        def add(i, _):
+            total = mine[i].astype(F32) + got[0, i].astype(F32)
+            mine[i] = (total + got[1, i].astype(F32) + got[2, i].astype(F32)).astype(BF16)
+            return 0
+
+        lax.fori_loop(0, 4, add, 0)
+        for j in (3, 2, 1):
             self.z_copy(j).start()
 
     def last(self):
@@ -782,27 +778,30 @@
 
     def finish(self):
         self.core_copy().wait_send()
-        for axis in (0, 1):
-            self.first_copy(axis).wait_send()
-            self.second_copy(axis).wait_send()
         for j in (1, 2, 3):
+            self.plane_copy(j).wait_send()
             self.z_copy(j).wait_send()
 
 
 def reduce_sems():
-    return [DMA((1,))] * 2 + [DMA((2,))] * 4 + [DMA((3,))] * 2
+    return [DMA((1,))] * 2 + [DMA((3,))] * 4
 
 
 def reduce_bufs(rows, width):
     shape = (rows, width)
-    return [
-        pltpu.VMEM((4, 2, 2) + shape, BF16),
-        pltpu.VMEM(split_shape((4, 2) + shape, 0), BF16),
-        pltpu.VMEM(split_shape((4, 2) + shape, 1), BF16),
-        pltpu.VMEM(split_shape((4,) + shape, 0), BF16),
-        pltpu.VMEM(split_shape((4,) + shape, 1), BF16),
-        pltpu.VMEM((3,) + shape, BF16),
-    ]
+    return [pltpu.VMEM(lead + shape, BF16) for lead in ((4, 2, 2), (3, 4), (3,))]
+
+
+MID_PARTS = 2
+
+
+def split_sum(ref, which):
+    width = ref.shape[-1]
+    cut = width // (MID_PARTS * 128) * 128
+    return ref.at[..., pl.ds(which * cut, (cut, width - cut)[which])]
+
+
+ORDER = (3, 1, 2, 0)
 
 
 class ReduceMid:
@@ -820,7 +819,7 @@
     def mine(self, zi, axis, other=0):
         z, x, y, c = self.place
         part = self.part.at[zi, :, abs(other - y), c] if axis == 0 else self.part.at[zi, abs(other - x), :, c]
-        return split_mid(part, axis)
+        return split_sum(part, axis)
 
     def first_copy(self, j, axis):
         z, x, y, c = self.place
@@ -830,8 +829,10 @@
 
     def z_copy(self, j, axis):
         z, x, y, c = self.place
+        there = (z ^ (2 if j == 2 else 1), x, y, c)
+        slot = {3: 0, 1: 1, 2: 2}[j]
         return remote(
-            self.mine(z ^ j, axis), self.got_z[axis].at[j - 1], self.zs.at[axis, j - 1], self.zr.at[axis, j - 1], (z ^ j, x, y, c)
+            self.mine(z ^ j, axis), self.got_z[axis].at[slot], self.zs.at[axis, slot], self.zr.at[axis, slot], there
         )
 
     def last_copy(self, axis):
@@ -840,13 +841,13 @@
             part, there = self.part.at[z, 1 - x, y, c], (z, 1 - x, y, c)
         else:
             part, there = self.part.at[z, x, 1 - y, c], (z, x, 1 - y, c)
-        return remote(split_mid(part, axis), split_mid(self.got_last, axis), self.ls.at[axis], self.lr.at[axis], there)
+        return remote(split_sum(part, axis), split_sum(self.got_last, axis), self.ls.at[axis], self.lr.at[axis], there)
 
     def send(self, j):
         self.core_copy(j).start()
 
     def send_all(self):
-        for j in (3, 2, 1, 0):
+        for j in ORDER:
             self.send(j)
 
     def first(self, j):
@@ -862,19 +863,25 @@
         for axis in (0, 1):
             self.first_copy(j, axis).wait_recv()
             add_into(self.mine(zi, axis), self.got_1[axis].at[zi], (2,))
-            if j:
+            if j % 2:
                 self.z_copy(j, axis).start()
 
+    def cross(self):
+        for axis in (0, 1):
+            self.z_copy(3, axis).wait_recv()
+            add_into(self.mine(self.place[0] ^ 2, axis), self.got_z[axis].at[0], (2,))
+            self.z_copy(2, axis).start()
+
     def fold(self):
         z, x, y, c = self.place
         for axis in (0, 1):
-            for j in (1, 2, 3):
+            for j in (1, 2):
                 self.z_copy(j, axis).wait_recv()
             mine, got = self.mine(z, axis), self.got_z[axis]
 
             def add(i, _, mine=mine, got=got):
-                total = mine[i].astype(F32) + got[0, i].astype(F32)
-                mine[i] = (total + got[1, i].astype(F32) + got[2, i].astype(F32)).astype(BF16)
+                total = mine[i].astype(F32) + got[1, i].astype(F32)
+                mine[i] = (total + got[2, i].astype(F32)).astype(BF16)
                 return 0
 
             lax.fori_loop(0, 2, add, 0)
@@ -902,7 +909,7 @@
 
 
 def reduce_mid_bufs(rows, width):
-    cut = width // 384 * 128
+    cut = width // (MID_PARTS * 128) * 128
     return [
         pltpu.VMEM((4, 2, 2, rows, width), BF16),
         pltpu.VMEM((4, 2, rows, cut), BF16),
@@ -915,6 +922,14 @@
 
 PIECES = 7
 GROUPS = 3
+
+
+def split_scratch(i, rest):
+    buf_count = [6, 6] + [3] * (PIECES - 2)
+    sem_count = [8, 8] + [6] * (PIECES - 2)
+    bufs, sems = rest[: sum(buf_count)], rest[sum(buf_count) :]
+    buf_at, sem_at = sum(buf_count[:i]), sum(sem_count[:i])
+    return bufs[buf_at : buf_at + buf_count[i]], sems[sem_at : sem_at + sem_count[i]]
 
 
 def backward_kernel(
@@ -928,7 +943,6 @@
     me = py * 2 + c
     length, feat = low.shape
     inner_width = act.shape[1]
-    bufs, sems = rest[: 6 * PIECES], rest[6 * PIECES :]
     slots_each = grads.shape[0] // 4
 
     sources = [(grads_in.at[i], grads.at[pl.ds(i * slots_each, slots_each)]) for i in range(4)]
@@ -969,8 +983,7 @@
     parts += [(Reduce, g_qkv.at[i], thirds(i)) for i in range(GROUPS)]
     parts += [(Reduce, g_small, whole(small_out))]
     sums_2, sum_1, sum_o, *sum_qkv, sum_small = reduces = [
-        kind(part, bufs[6 * i : 6 * i + 6], sems[8 * i : 8 * i + 8], place, write)
-        for i, (kind, part, write) in enumerate(parts)
+        kind(part, *split_scratch(i, rest), place, write) for i, (kind, part, write) in enumerate(parts)
     ]
 
     sums[...] = jnp.zeros_like(sums)
@@ -1003,14 +1016,14 @@
     loads[5].wait()
 
     def outer_grad(i, _):
-        j = 3 - i
+        j = jnp.where(i == 1, 1, jnp.where(i == 2, 2, 3 - i))
         zi = z ^ j
         width = inner_width // 4
         part = dot_rows(act[:, block_of(zi, width)], second[...])
         g_2[zi] = part.astype(BF16).reshape(g_2.shape[1:])
         sums_2.send(j)
         for k in (1, 2, 3):
-            pl.when(i == k)(in_order((sums_2.first, 4 - k)))
+            pl.when(i == k)(in_order((sums_2.first, ORDER[k - 1])))
         return 0
 
     lax.fori_loop(0, 4, outer_grad, 0)
@@ -1018,7 +1031,7 @@
     for copy in loads[6:9]:
         copy.wait()
     turned[...] = low[...].T
-    under_inner = {5: [(sums_2.turn, 3)], 10: [(sums_2.turn, 2)]}
+    under_inner = {8: [(sums_2.turn, 3)]}
 
     def inner_grad(i, _):
         block = block_of(i, TILE)
@@ -1051,7 +1064,7 @@
         return 0
 
     lax.fori_loop(0, 2, hidden_grad, 0)
-    in_order((sum_1.first, 3), (sum_1.first, 2), (sums_2.turn, 1))()
+    in_order((sum_1.first, 3), (sum_1.first, 1), (sums_2.turn, 1))()
     first = second
 
     def norm_one(i, _):
@@ -1067,7 +1080,7 @@
         return 0
 
     lax.fori_loop(0, length // rows, norm_one, 0)
-    in_order((sum_1.first, 1), (sum_1.first, 0))()
+    in_order((sum_1.first, 2), (sum_1.first, 0), (sums_2.turn, 2), (sums_2.cross,))()
     for copy in slabs:
         copy.wait()
     g_o[...] = dot_rows(att[...], first[...]).astype(BF16).reshape(g_o.shape)
@@ -1111,13 +1124,11 @@
         d_qkv[:, pl.ds(2 * feat + start, 128)] = jnp.where(low_lane, v_0, v_1).astype(BF16)
 
     under = {
-        2: [(sum_1.turn, 3)],
-        4: [(sum_1.turn, 2)],
-        5: [(sum_qkv[0].first,)],
-        7: [(sum_1.turn, 1)],
-        9: [(sums_2.fold,), (sum_qkv[1].first,)],
-        10: [(sum_1.turn, 0)],
-        11: [(sums_2.last,)],
+        4: [(sums_2.fold,)],
+        5: [(sum_1.turn, 3), (sum_qkv[0].first,)],
+        8: [(sums_2.last,), (sum_1.turn, 1)],
+        9: [(sum_qkv[1].first,)],
+        10: [(sum_1.turn, 2), (sum_1.cross,)],
     }
 
     def group(i, _):
@@ -1137,48 +1148,42 @@
         return 0
 
     lax.fori_loop(0, GROUPS, group, 0)
+    thirds_0, thirds_1, thirds_2 = sum_qkv
+    in_order((sum_1.turn, 0), (sum_1.fold,), (sum_o.along_z,))()
     tally(0, d_qkv[:, 0:feat].astype(F32))
     tally(1, d_qkv[:, 2 * feat : 3 * feat].astype(F32))
+    thirds_2.first()
     g_small[:, :, :, :, 0:8, :] = pack_rows(sums[...], feat // 32, 32).reshape(4, 2, 2, 2, 8, 128)
     for i in range(4):
         part = sums1[:, i * (inner_width // 4) : (i + 1) * (inner_width // 4)]
         g_small[i, :, :, :, 8:16, :] = pack_rows(part, inner_width // 32, 8).reshape(2, 2, 2, 8, 128)
     sum_small.send_all()
-    sum_qkv[2].first()
+    grad_tokens = x.reshape(4, length // 4, feat)
+    token_copies = [page_copy(grad_tokens, tokens_out, ts, tr, j) for j in range(3)]
+    token_own = pltpu.make_async_copy(grad_tokens.at[me], tokens_out.at[me], local.at[19])
 
     def token_grad(i, _):
-        block = block_of(i, rows)
+        block = block_of(me ^ (3 - i), length // 4)
         total = grad[block, :]
         for t in range(3):
             total += dot_cols(
                 d_qkv[block, t * feat : (t + 1) * feat], wb[(t + 1) * feat : (t + 2) * feat, :]
             )
         x[block, :] = total.astype(BF16)
-        return 0
-
-    lax.fori_loop(0, length // rows, token_grad, 0)
-    grad_tokens = x.reshape(4, length // 4, feat)
-    token_copies = [page_copy(grad_tokens, tokens_out, ts, tr, j) for j in range(3)]
-    for copy in token_copies:
-        copy.start()
-    token_own = pltpu.make_async_copy(grad_tokens.at[me], tokens_out.at[me], local.at[19])
+        for j in range(3):
+            pl.when(i == 2 - j)(in_order((token_copies[j].start,)))
+        return 0
+
+    lax.fori_loop(0, 4, token_grad, 0)
     token_own.start()
-    thirds_0, thirds_1, thirds_2 = sum_qkv
     in_order(
         (sum_small.first,),
-        (sum_o.second,),
-        (thirds_0.second,),
-        (sum_o.along_z,),
-        (thirds_1.second,),
         (thirds_0.along_z,),
-        (sum_small.second,),
-        (sum_1.fold,),
-        (thirds_2.second,),
         (thirds_1.along_z,),
+        (sum_1.last,),
+        (sum_o.last,),
         (sum_small.along_z,),
-        (sum_o.last,),
         (thirds_2.along_z,),
-        (sum_1.last,),
         (thirds_0.last,),
         (thirds_1.last,),
         (sum_small.last,),
@@ -1246,23 +1251,19 @@
     )(*saved, *weights, grad_pages, layer_slots, slots, live)
 
 
-def small_shard(weights):
-    rows = []
-    for i in SMALL_ORDER:
-        rows += [weights[i], jnp.zeros((128 - weights[i].shape[0],), BF16)]
-    rows.append(jnp.zeros((128 * (16 - len(SMALL_ORDER)),), BF16))
-    return jnp.concatenate(rows).reshape(16, 128)
-
-
+LARGE = (0, 2, 3, 5, 9, 11)
 SMALL_ORDER = (1, 4, 6, 7, 8, 12, 13, 14, 10)
 
 
-def finish_kernel(count, *refs):
-    ins, outs, stages, sems = refs[:count], refs[count : 2 * count], refs[2 * count : 3 * count], refs[3 * count]
+def finish_kernel(count, sizes, *refs):
+    ins, small, outs = refs[:count], refs[count], refs[count + 1 : 2 * count + 1]
+    vectors, stages, sems = refs[2 * count + 1 :][: len(sizes)], refs[-count - 1 : -1], refs[-1]
     inward = [pltpu.make_async_copy(i, s, sems.at[0, n]) for n, (i, s) in enumerate(zip(ins, stages))]
     outward = [pltpu.make_async_copy(s, o, sems.at[1, n]) for n, (s, o) in enumerate(zip(stages, outs))]
     for copy in inward:
         copy.start()
+    for row, (size, ref) in enumerate(zip(sizes, vectors)):
+        ref[...] = small[row : row + 1, 0:size].reshape(size)
     for first, second in zip(inward, outward):
         first.wait()
         second.start()
@@ -1270,37 +1271,36 @@
         copy.wait()
 
 
-def finish(arrays):
+def finish(arrays, small, sizes):
     count = len(arrays)
     anywhere = pl.BlockSpec(memory_space=pl.ANY)
+    vmem = pl.BlockSpec(memory_space=pltpu.VMEM)
 
     def body(*refs):
-        finish_kernel(count, *refs)
+        finish_kernel(count, sizes, *refs)
 
     return pl.pallas_call(
         body,
-        out_shape=[jax.ShapeDtypeStruct(a.shape, a.dtype) for a in arrays],
-        in_specs=[anywhere] * count,
-        out_specs=[anywhere] * count,
+        out_shape=[jax.ShapeDtypeStruct(a.shape, a.dtype) for a in arrays]
+        + [jax.ShapeDtypeStruct((size,), F32) for size in sizes],
+        in_specs=[anywhere] * count + [vmem],
+        out_specs=[anywhere] * count + [vmem] * len(sizes),
         scratch_shapes=[pltpu.VMEM(a.shape, a.dtype) for a in arrays] + [DMA((2, count))],
         compiler_params=pltpu.CompilerParams(vmem_limit_bytes=VMEM_LIMIT),
         name="finish",
-    )(*arrays)
+    )(*arrays, small)
 
 
 def by_kernels(tokens, band_ids, page_mask, weights, grad_output):
-    large = [weights[i] for i in (0, 2, 3, 5, 9, 11)]
-    got = forward(tokens, grad_output, band_ids, page_mask, *large, small_shard(weights))
+    large = [weights[i] for i in LARGE]
+    vectors = [weights[i] for i in SMALL_ORDER]
+    got = forward(vectors, tokens, grad_output, band_ids, page_mask, *large)
     saved, full, (grad_slots, layer_slots, slots, live) = got[:11], got[11:17], got[17:]
     full = [w if i == 4 else w.reshape(-1, w.shape[-1]) for i, w in enumerate(full)]
     sums = backward(saved, full, grad_slots, layer_slots, slots, live, tokens.shape)
-    grads = [None] * len(weights)
-    for row, i in enumerate(SMALL_ORDER):
-        grads[i] = sums[8][row, : weights[i].shape[0]]
-    sums = finish(sums[:8])
-    for i, total in zip((0, 2, 3, 5, 9, 11), sums[2:]):
-        grads[i] = total
-    return tuple(sums[:2]) + tuple(grads)
+    results = finish(sums[:8], sums[8], [v.shape[0] for v in vectors])
+    grads = dict(zip(LARGE + SMALL_ORDER, results[2:]))
+    return tuple(results[:2]) + tuple(grads[i] for i in range(len(weights)))
 
 
 def per_device(hand_made, *args):

time: 217 us -> 203 us (0.935)
  Pallas kernels: 209 us -> 201 us
  local copies, waits for them, and re-layouts: 7.76 us -> 0 us
    pallas_call x1, Pallas kernels: 113 us -> 104 us  [backward(): pl.pallas_call(backward_kernel, out_shape=[jax.ShapeDtypeStruct(shape, ki...]
    concatenate x1 -> x0, local copies, waits for them, and re-layouts: 6.69 us -> none  [small_shard(): return jnp.concatenate(rows).reshape(16, 128)]
where the time goes in v2:
time: 203 us; the launch traced here: 202 us
  Pallas kernels  201 us (99%)
    pallas_call x1, Pallas kernels, backward(): pl.pallas_call(backward_kernel, out_shape=[jax.ShapeDtypeStruct(shape, ki...  104 us
    pallas_call x1, Pallas kernels, forward(): pl.pallas_call(forward_kernel, out_shape=[jax.ShapeDtypeStruct(shape, kin...  92.9 us
    pallas_call x1, Pallas kernels, finish(): pl.pallas_call(body, out_shape=[jax.ShapeDtypeStruct(a.shape, a.dtype) fo...  4.49 us

profile of v2, /device:TPU:0, one launch (start us, length us, event | category | flops | bytes accessed | tf_op | source)
XLA Modules:
  0.0 201.8 jit_solution(10413691893451163277)
XLA Ops:
  0.7 92.9 %forward.1 = (bf16[512,2304]{1,0:T(8,128)(2,1)}, f32[16,512]{1,0:T(8,128)}, bf16[512,768]{1,0:T(8,128)(2,1)}, bf16[512,768]{1,0:T(8,128)(2,1)}, f32[512,768]{1,0...) custom-call(bf16[24]{0:T(256)(128)(2,1)} %refs_0_.1, ...), custom_call_target="tpu_custom_call" | custom-call | tf_op jit(solution)/shard_map/forward/pallas_call | solution.py:670
  93.6 103.6 %backward.1 = (bf16[4,256,768]{2,1,0:T(8,128)(2,1)}, bf16[4,128,768]{2,1,0:T(8,128)(2,1)}, f32[24,768]{1,0:T(8,128)}, f32[24,768]{1,0:T(8,128)}, f32[24,768]{1,0...) custom-call(bf16[512,2304]{1,0:T(8,128)(2,1)} %get-tuple-element.64.qkv_in, ...), custom_call_target="tpu_custom_call" | custom-call | tf_op jit(solution)/shard_map/backward/pallas_call | solution.py:1238
  197.2 4.5 %finish.1 = (bf16[4,256,768]{2,1,0:T(8,128)(2,1)}, bf16[4,128,768]{2,1,0:T(8,128)(2,1)}, f32[24,768]{1,0:T(8,128)}, f32[24,768]{1,0:T(8,128)}, f32[24,768]{1,0:T...) custom-call(bf16[4,256,768]{2,1,0:T(8,128)(2,1)} %get-tuple-element., ...), custom_call_target="tpu_custom_call" | custom-call | tf_op jit(solution)/shard_map/finish/pallas_call | solution.py:1282

commit v3 on v2

--- a/solution.py
+++ b/solution.py
@@ -298,8 +298,10 @@
 
     def z_copy(self, j):
         z, x, y, c = self.place
-        there = (z ^ j, x, y, c)
-        return remote(self.own, self.buf.at[z, x, y, c], self.zs.at[j - 1], self.zr.at[j - 1], there)
+        zi = z ^ (2 if j == 3 else 0)
+        source = self.buf.at[zi, x, y, c] if j == 3 else self.own
+        there = (z ^ (2 if j == 2 else 1), x, y, c)
+        return remote(source, self.buf.at[zi, x, y, c], self.zs.at[j - 1], self.zr.at[j - 1], there)
 
     def side_copy(self, axis):
         z, x, y, c = self.place
@@ -309,9 +311,11 @@
 
     def half_copy(self, j, axis):
         z, x, y, c = self.place
-        part = self.buf.at[z, 1 - x, y, c] if axis == 0 else self.buf.at[z, x, 1 - y, c]
+        zi = z ^ (2 if j == 3 else 0)
+        part = self.buf.at[zi, 1 - x, y, c] if axis == 0 else self.buf.at[zi, x, 1 - y, c]
         part = split_mid(part, axis)
-        return remote(part, part, self.hs.at[axis, j - 1], self.hr.at[axis, j - 1], (z ^ j, x, y, c))
+        there = (z ^ (2 if j == 2 else 1), x, y, c)
+        return remote(part, part, self.hs.at[axis, j - 1], self.hr.at[axis, j - 1], there)
 
     def far_copy(self, j, axis):
         z, x, y, c = self.place
@@ -322,49 +326,51 @@
         part = split_mid(part, axis)
         return remote(part, part, self.fs.at[axis, j], self.fr.at[axis, j], there)
 
-    def core_copy(self, k):
-        z, x, y, c = self.place
-        part = self.buf.at[:, (x, 1 - x, x, 1 - x)[k], (y, y, 1 - y, 1 - y)[k], c]
-        return remote(part, part, self.cs.at[k], self.cr.at[k], (z, x, y, 1 - c))
+    def core_copy(self, j):
+        z, x, y, c = self.place
+        part = self.buf.at[z ^ j, :, :, c]
+        return remote(part, part, self.cs.at[j], self.cr.at[j], (z, x, y, 1 - c))
 
     def start(self):
         for axis in (0, 1):
             self.side_copy(axis).start()
-        for j in (1, 2, 3):
+        for j in (2, 1):
             self.z_copy(j).start()
 
     def turn(self):
         for axis in (0, 1):
             self.side_copy(axis).wait_recv()
-            for j in (1, 2, 3):
+            for j in (2, 1):
                 self.half_copy(j, axis).start()
         for axis in (0, 1):
             self.far_copy(0, axis).start()
 
     def far(self, j):
         self.z_copy(j).wait_recv()
+        if j == 2:
+            self.z_copy(3).start()
         for axis in (0, 1):
             self.half_copy(j, axis).wait_recv()
+            if j == 2:
+                self.half_copy(3, axis).start()
             self.far_copy(j, axis).start()
 
-    def core(self, k):
-        if k:
-            for j in range(4):
-                for axis in (0, 1):
-                    self.far_copy(j, axis).wait_recv()
-            for k in (1, 2, 3):
-                self.core_copy(k).start()
-        else:
-            self.core_copy(0).start()
+    def core(self, j):
+        for axis in (0, 1):
+            self.far_copy(j, axis).wait_recv()
+        self.core_copy(j).start()
 
     def steps(self):
         far, core = self.far, self.core
         return [
             in_order((self.turn,)),
+            in_order((far, 2)),
             in_order((far, 1)),
-            in_order((far, 2)),
-            in_order((far, 3), (core, 0)),
+            in_order((far, 3)),
+            in_order((core, 0)),
+            in_order((core, 2)),
             in_order((core, 1)),
+            in_order((core, 3)),
         ]
 
     def arrive(self):
@@ -484,10 +490,10 @@
     token_copies = [page_copy(tokens, x_buf, ts, tr, j) for j in range(3)]
     grad_copies = [page_copy(grads, grad_pages, gs, gr, j) for j in range(3)]
     gathers = [
-        kind(own, buf, sems[8 * i :][: 8 if kind is Gather else 10], place)
+        kind(own, buf, sems[(0, 8, 16, 26)[i] :][: 8 if kind is Gather else 10], place)
         for i, (kind, own, buf) in enumerate(
             [(Gather, small.at[here], small), (Gather, a_buf.at[here], a_buf)]
-            + [(Gather, w_1, w1_buf), (GatherMid, w_2, w2_buf)]
+            + [(GatherMid, w_1, w1_buf), (GatherMid, w_2, w2_buf)]
         )
     ]
     vectors, atts, inner, outer = gathers
@@ -497,8 +503,6 @@
     vectors.start()
     for copy in token_copies:
         copy.start()
-    inner.start()
-    outer.start()
     slot_cap = grads.shape[1]
     hot = (rows_of((8, length)) == ids[pl.ds(me, 1), :]).astype(F32)
     earlier = (rows_of((length, length)) < lanes((length, length))).astype(BF16)
@@ -506,13 +510,11 @@
     slots[...] = jnp.sum(hot * rank, axis=0, keepdims=True).astype(jnp.int32)
     live[...] = jnp.broadcast_to(mask[pl.ds(me, 1), :].astype(F32), (8, length)).T[:, 0:1]
     steps_0, steps_1, steps_2 = atts.steps(), inner.steps(), outer.steps()
-    behind = {3: [steps_1[0]], 4: [steps_1[1]], 5: [steps_1[2], steps_2[0]], 6: [steps_1[3]]}
+    own = in_order(*[(copy.wait,) for copy in copies[4:6]])
+    behind = {1: [inner.start], 3: [own, steps_1[0]], 4: [outer.start], 6: [steps_1[1]]}
     for i, (main, extra) in enumerate(zip(steps_0, vectors.steps())):
         main()
         extra()
-        if i == 3:
-            for copy in copies[4:6]:
-                copy.wait()
         for step in behind.get(i, ()):
             step()
     for copy in copies[6:]:
@@ -533,7 +535,7 @@
     for i, ref in enumerate((q_out, k_out, v_out, o_out)):
         out.send(a_buf.at[:, :, :, :, :, pl.ds(i * feat, feat)], ref)
     out.send(x_rows, x_out)
-    steps_1[4]()
+    steps_1[2]()
 
     def project(j, _):
         start = pl.multiple_of(j * TILE, TILE)
@@ -546,8 +548,9 @@
 
     lax.fori_loop(0, 3 * feat // TILE, project, 0)
     out.send(qkv, qkv_out)
-    steps_1[5]()
-    under = {0: steps_1[6], 2: steps_1[7], 3: steps_2[1], 6: steps_2[2], 9: steps_2[3]}
+    steps_2[0]()
+    under = {2: steps_1[3], 4: steps_2[1], 6: steps_1[4], 7: steps_2[2], 8: steps_1[5]}
+    under |= {9: steps_1[6], 10: steps_1[7], 11: steps_2[3]}
     scale = HEAD_DIM**-0.5
 
     def pair(p, _):
@@ -603,16 +606,29 @@
     lax.fori_loop(0, inner_width // TILE, ffn_in, 0)
     out.send(act, act_out)
     out.send(slope, slope_out)
+    chunk = inner_width // 4
+
+    def add_chunk(j):
+        outer.core_copy(j).wait_recv()
+        zi = z ^ j
+
+        def part(i, _):
+            block = block_of(i, TILE)
+            more = dot(act[:, block_of(zi, chunk)], w2_buf[zi, :, :, :, :, block].reshape(chunk, TILE))
+            second[:, block] = more if j == 0 else second[:, block] + more
+            return 0
+
+        lax.fori_loop(0, feat // TILE, part, 0)
+
     steps_2[4]()
-    outer.arrive()
+    steps_2[5]()
+    add_chunk(0)
+    steps_2[6]()
+    add_chunk(2)
+    steps_2[7]()
+    add_chunk(1)
+    add_chunk(3)
     out.send(w2_buf, w2_out)
-
-    def ffn_out(j, _):
-        block = block_of(j, TILE)
-        second[:, block] = dot(act[...], columns(w2_buf, block.start, TILE))
-        return 0
-
-    lax.fori_loop(0, feat // TILE, ffn_out, 0)
 
     def norm_two(i, _):
         block = block_of(i, rows)
@@ -696,8 +712,8 @@
             DMA((3,)),
             DMA((14,)),
         ]
-        + gather_sems() * 3
-        + mid_sems(),
+        + gather_sems() * 2
+        + mid_sems() * 2,
         compiler_params=pltpu.CompilerParams(
             collective_id=0, has_side_effects=True, vmem_limit_bytes=VMEM_LIMIT
         ),

time: 203 us -> 194 us (0.956)
  Pallas kernels: 201 us -> 193 us
    pallas_call x1, Pallas kernels: 104 us -> 97.1 us  [backward(): pl.pallas_call(backward_kernel, out_shape=[jax.ShapeDtypeStruct(shape, ki...]
where the time goes in v3:
time: 194 us
  Pallas kernels  193 us (99%)
    pallas_call x1, Pallas kernels, backward(): pl.pallas_call(backward_kernel, out_shape=[jax.ShapeDtypeStruct(shape, ki...  97.1 us
    pallas_call x1, Pallas kernels, forward(): pl.pallas_call(forward_kernel, out_shape=[jax.ShapeDtypeStruct(shape, kin...  91.5 us
    pallas_call x1, Pallas kernels, finish(): pl.pallas_call(body, out_shape=[jax.ShapeDtypeStruct(a.shape, a.dtype) fo...  4.49 us

profile of v3, /device:TPU:0, one launch (start us, length us, event | category | flops | bytes accessed | tf_op | source)
XLA Modules:
  0.0 193.9 jit_solution(6732551985239253384)
XLA Ops:
  0.7 91.5 %forward.1 = (bf16[512,2304]{1,0:T(8,128)(2,1)}, f32[16,512]{1,0:T(8,128)}, bf16[512,768]{1,0:T(8,128)(2,1)}, bf16[512,768]{1,0:T(8,128)(2,1)}, f32[512,768]{1,0...) custom-call(bf16[24]{0:T(256)(128)(2,1)} %refs_0_.1, ...), custom_call_target="tpu_custom_call" | custom-call | tf_op jit(solution)/shard_map/forward/pallas_call | solution.py:686
  92.1 97.1 %backward.1 = (bf16[4,256,768]{2,1,0:T(8,128)(2,1)}, bf16[4,128,768]{2,1,0:T(8,128)(2,1)}, f32[24,768]{1,0:T(8,128)}, f32[24,768]{1,0:T(8,128)}, f32[24,768]{1,0...) custom-call(bf16[512,2304]{1,0:T(8,128)(2,1)} %get-tuple-element.64.qkv_in, ...), custom_call_target="tpu_custom_call" | custom-call | tf_op jit(solution)/shard_map/backward/pallas_call | solution.py:1254
  189.3 4.5 %finish.1 = (bf16[4,256,768]{2,1,0:T(8,128)(2,1)}, bf16[4,128,768]{2,1,0:T(8,128)(2,1)}, f32[24,768]{1,0:T(8,128)}, f32[24,768]{1,0:T(8,128)}, f32[24,768]{1,0:T...) custom-call(bf16[4,256,768]{2,1,0:T(8,128)(2,1)} %get-tuple-element., ...), custom_call_target="tpu_custom_call" | custom-call | tf_op jit(solution)/shard_map/finish/pallas_call | solution.py:1298

commit v4 on v3

--- a/solution.py
+++ b/solution.py
@@ -549,8 +549,7 @@
     lax.fori_loop(0, 3 * feat // TILE, project, 0)
     out.send(qkv, qkv_out)
     steps_2[0]()
-    under = {2: steps_1[3], 4: steps_2[1], 6: steps_1[4], 7: steps_2[2], 8: steps_1[5]}
-    under |= {9: steps_1[6], 10: steps_1[7], 11: steps_2[3]}
+    under = {3: steps_1[3], 5: steps_2[1], 8: steps_1[4], 9: steps_2[2], 10: steps_1[5], 11: steps_1[6]}
     scale = HEAD_DIM**-0.5
 
     def pair(p, _):
@@ -578,6 +577,8 @@
 
     lax.fori_loop(0, pairs, pair, 0)
     out.send(att, att_out)
+    steps_1[7]()
+    steps_2[3]()
     rows = 128
 
     def norm_one(i, _):
@@ -808,7 +809,7 @@
     return [pltpu.VMEM(lead + shape, BF16) for lead in ((4, 2, 2), (3, 4), (3,))]
 
 
-MID_PARTS = 2
+MID_PARTS = 3
 
 
 def split_sum(ref, which):
@@ -1165,15 +1166,11 @@
 
     lax.fori_loop(0, GROUPS, group, 0)
     thirds_0, thirds_1, thirds_2 = sum_qkv
-    in_order((sum_1.turn, 0), (sum_1.fold,), (sum_o.along_z,))()
+    sum_1.turn(0)
     tally(0, d_qkv[:, 0:feat].astype(F32))
     tally(1, d_qkv[:, 2 * feat : 3 * feat].astype(F32))
     thirds_2.first()
-    g_small[:, :, :, :, 0:8, :] = pack_rows(sums[...], feat // 32, 32).reshape(4, 2, 2, 2, 8, 128)
-    for i in range(4):
-        part = sums1[:, i * (inner_width // 4) : (i + 1) * (inner_width // 4)]
-        g_small[i, :, :, :, 8:16, :] = pack_rows(part, inner_width // 32, 8).reshape(2, 2, 2, 8, 128)
-    sum_small.send_all()
+    in_order((sum_1.fold,), (sum_o.along_z,))()
     grad_tokens = x.reshape(4, length // 4, feat)
     token_copies = [page_copy(grad_tokens, tokens_out, ts, tr, j) for j in range(3)]
     token_own = pltpu.make_async_copy(grad_tokens.at[me], tokens_out.at[me], local.at[19])
@@ -1191,6 +1188,11 @@
         return 0
 
     lax.fori_loop(0, 4, token_grad, 0)
+    g_small[:, :, :, :, 0:8, :] = pack_rows(sums[...], feat // 32, 32).reshape(4, 2, 2, 2, 8, 128)
+    for i in range(4):
+        part = sums1[:, i * (inner_width // 4) : (i + 1) * (inner_width // 4)]
+        g_small[i, :, :, :, 8:16, :] = pack_rows(part, inner_width // 32, 8).reshape(2, 2, 2, 8, 128)
+    sum_small.send_all()
     token_own.start()
     in_order(
         (sum_small.first,),

time: 194 us -> 189 us (0.974)
  Pallas kernels: 193 us -> 188 us
    pallas_call x1, Pallas kernels: 97.1 us -> 93.1 us  [backward(): pl.pallas_call(backward_kernel, out_shape=[jax.ShapeDtypeStruct(shape, ki...]
where the time goes in v4:
time: 189 us
  Pallas kernels  188 us (99%)
    pallas_call x1, Pallas kernels, backward(): pl.pallas_call(backward_kernel, out_shape=[jax.ShapeDtypeStruct(shape, ki...  93.1 us
    pallas_call x1, Pallas kernels, forward(): pl.pallas_call(forward_kernel, out_shape=[jax.ShapeDtypeStruct(shape, kin...  90.6 us
    pallas_call x1, Pallas kernels, finish(): pl.pallas_call(body, out_shape=[jax.ShapeDtypeStruct(a.shape, a.dtype) fo...  4.49 us

profile of v4, /device:TPU:0, one launch (start us, length us, event | category | flops | bytes accessed | tf_op | source)
XLA Modules:
  0.0 189.0 jit_solution(17262983316583108346)
XLA Ops:
  0.7 90.6 %forward.1 = (bf16[512,2304]{1,0:T(8,128)(2,1)}, f32[16,512]{1,0:T(8,128)}, bf16[512,768]{1,0:T(8,128)(2,1)}, bf16[512,768]{1,0:T(8,128)(2,1)}, f32[512,768]{1,0...) custom-call(bf16[24]{0:T(256)(128)(2,1)} %refs_0_.1, ...), custom_call_target="tpu_custom_call" | custom-call | tf_op jit(solution)/shard_map/forward/pallas_call | solution.py:687
  91.3 93.1 %backward.1 = (bf16[4,256,768]{2,1,0:T(8,128)(2,1)}, bf16[4,128,768]{2,1,0:T(8,128)(2,1)}, f32[24,768]{1,0:T(8,128)}, f32[24,768]{1,0:T(8,128)}, f32[24,768]{1,0...) custom-call(bf16[512,2304]{1,0:T(8,128)(2,1)} %get-tuple-element.64.qkv_in, ...), custom_call_target="tpu_custom_call" | custom-call | tf_op jit(solution)/shard_map/backward/pallas_call | solution.py:1256
  184.4 4.5 %finish.1 = (bf16[4,256,768]{2,1,0:T(8,128)(2,1)}, bf16[4,128,768]{2,1,0:T(8,128)(2,1)}, f32[24,768]{1,0:T(8,128)}, f32[24,768]{1,0:T(8,128)}, f32[24,768]{1,0:T...) custom-call(bf16[4,256,768]{2,1,0:T(8,128)(2,1)} %get-tuple-element., ...), custom_call_target="tpu_custom_call" | custom-call | tf_op jit(solution)/shard_map/finish/pallas_call | solution.py:1300

commit v5 on v4

--- a/solution.py
+++ b/solution.py
@@ -178,18 +178,10 @@
 
 def split_ref(ref, which):
     rows, width = ref.shape[-2:]
-    cut = width // 6
+    cut = width // 3
     if cut % 128:
         return ref.at[..., pl.ds(which * (rows // 2), rows // 2), :]
     return ref.at[..., pl.ds(which * cut, (cut, width - cut)[which])]
-
-
-def split_shape(shape, which):
-    rows, width = shape[-2:]
-    cut = width // 6
-    if cut % 128:
-        return shape[:-2] + (rows // 2, width)
-    return shape[:-1] + ((cut, width - cut)[which],)
 
 
 def in_order(*calls):
@@ -287,7 +279,7 @@
 
 def split_mid(ref, which):
     width = ref.shape[-1]
-    cut = width // 384 * 128
+    cut = width // 640 * 128
     return ref.at[..., pl.ds(which * cut, (cut, width - cut)[which])]
 
 

time: 189 us -> 186 us (0.984)
  Pallas kernels: 188 us -> 185 us
    pallas_call x1, Pallas kernels: 90.6 us -> 86.5 us  [forward(): pl.pallas_call(forward_kernel, out_shape=[jax.ShapeDtypeStruct(shape, kin...]
where the time goes in v5:
time: 186 us
  Pallas kernels  185 us (99%)
    pallas_call x1, Pallas kernels, backward(): pl.pallas_call(backward_kernel, out_shape=[jax.ShapeDtypeStruct(shape, ki...  93.9 us
    pallas_call x1, Pallas kernels, forward(): pl.pallas_call(forward_kernel, out_shape=[jax.ShapeDtypeStruct(shape, kin...  86.5 us
    pallas_call x1, Pallas kernels, finish(): pl.pallas_call(body, out_shape=[jax.ShapeDtypeStruct(a.shape, a.dtype) fo...  4.49 us

profile of v5, /device:TPU:0, one launch (start us, length us, event | category | flops | bytes accessed | tf_op | source)
XLA Modules:
  0.0 185.7 jit_solution(12335011155599679180)
XLA Ops:
  0.7 86.5 %forward.1 = (bf16[512,2304]{1,0:T(8,128)(2,1)}, f32[16,512]{1,0:T(8,128)}, bf16[512,768]{1,0:T(8,128)(2,1)}, bf16[512,768]{1,0:T(8,128)(2,1)}, f32[512,768]{1,0...) custom-call(bf16[24]{0:T(256)(128)(2,1)} %refs_0_.1, ...), custom_call_target="tpu_custom_call" | custom-call | tf_op jit(solution)/shard_map/forward/pallas_call | solution.py:679
  87.2 93.9 %backward.1 = (bf16[4,256,768]{2,1,0:T(8,128)(2,1)}, bf16[4,128,768]{2,1,0:T(8,128)(2,1)}, f32[24,768]{1,0:T(8,128)}, f32[24,768]{1,0:T(8,128)}, f32[24,768]{1,0...) custom-call(bf16[512,2304]{1,0:T(8,128)(2,1)} %get-tuple-element.64.qkv_in, ...), custom_call_target="tpu_custom_call" | custom-call | tf_op jit(solution)/shard_map/backward/pallas_call | solution.py:1248
  181.1 4.5 %finish.1 = (bf16[4,256,768]{2,1,0:T(8,128)(2,1)}, bf16[4,128,768]{2,1,0:T(8,128)(2,1)}, f32[24,768]{1,0:T(8,128)}, f32[24,768]{1,0:T(8,128)}, f32[24,768]{1,0:T...) custom-call(bf16[4,256,768]{2,1,0:T(8,128)(2,1)} %get-tuple-element., ...), custom_call_target="tpu_custom_call" | custom-call | tf_op jit(solution)/shard_map/finish/pallas_call | solution.py:1292

commit v6 on v5

--- a/solution.py
+++ b/solution.py
@@ -571,7 +571,7 @@
     out.send(att, att_out)
     steps_1[7]()
     steps_2[3]()
-    rows = 128
+    rows = 256
 
     def norm_one(i, _):
         block = block_of(i, rows)
@@ -1003,7 +1003,7 @@
 
     for copy in loads[:5]:
         copy.wait()
-    rows = 128
+    rows = 256
 
     def norm_two(i, _):
         block = block_of(i, rows)

time: 186 us -> 186 us (level)
  no operation moved by 1% of the time
where the time goes in v6:
time: 186 us; the launch traced here: 185 us
  Pallas kernels  185 us (99%)
    pallas_call x1, Pallas kernels, backward(): pl.pallas_call(backward_kernel, out_shape=[jax.ShapeDtypeStruct(shape, ki...  93.9 us
    pallas_call x1, Pallas kernels, forward(): pl.pallas_call(forward_kernel, out_shape=[jax.ShapeDtypeStruct(shape, kin...  86.2 us
    pallas_call x1, Pallas kernels, finish(): pl.pallas_call(body, out_shape=[jax.ShapeDtypeStruct(a.shape, a.dtype) fo...  4.49 us

profile of v6, /device:TPU:0, one launch (start us, length us, event | category | flops | bytes accessed | tf_op | source)
XLA Modules:
  0.0 185.4 jit_solution(17353055813996429198)
XLA Ops:
  0.7 86.2 %forward.1 = (bf16[512,2304]{1,0:T(8,128)(2,1)}, f32[16,512]{1,0:T(8,128)}, bf16[512,768]{1,0:T(8,128)(2,1)}, bf16[512,768]{1,0:T(8,128)(2,1)}, f32[512,768]{1,0...) custom-call(bf16[24]{0:T(256)(128)(2,1)} %refs_0_.1, ...), custom_call_target="tpu_custom_call" | custom-call | tf_op jit(solution)/shard_map/forward/pallas_call | solution.py:679
  86.9 93.9 %backward.1 = (bf16[4,256,768]{2,1,0:T(8,128)(2,1)}, bf16[4,128,768]{2,1,0:T(8,128)(2,1)}, f32[24,768]{1,0:T(8,128)}, f32[24,768]{1,0:T(8,128)}, f32[24,768]{1,0...) custom-call(bf16[512,2304]{1,0:T(8,128)(2,1)} %get-tuple-element.64.qkv_in, ...), custom_call_target="tpu_custom_call" | custom-call | tf_op jit(solution)/shard_map/backward/pallas_call | solution.py:1248
  180.8 4.5 %finish.1 = (bf16[4,256,768]{2,1,0:T(8,128)(2,1)}, bf16[4,128,768]{2,1,0:T(8,128)(2,1)}, f32[24,768]{1,0:T(8,128)}, f32[24,768]{1,0:T(8,128)}, f32[24,768]{1,0:T...) custom-call(bf16[4,256,768]{2,1,0:T(8,128)(2,1)} %get-tuple-element., ...), custom_call_target="tpu_custom_call" | custom-call | tf_op jit(solution)/shard_map/finish/pallas_call | solution.py:1292
